TPU v7x, 512 devices: a whole 4x8x8 slice. The times are simulated.
512 devices in a mesh: shot: 32 (over y_hi, z, core), slab: 16 (over x, y_lo).
Axes of the slice: x: 4, y: 8 (y_hi: 2, y_lo: 4; y = y_hi * 4 + y_lo), z: 8, core: 2. Of those that a mesh axis runs over, the one named last changes fastest.
Arguments:
- previous_field: bfloat16 [32, 128, 32, 128], P('shot', 'slab'), may hold values from -6 to 6
- current_field: bfloat16 [32, 128, 32, 128], P('shot', 'slab'), may hold values from -6 to 6
- adjoint_next: bfloat16 [32, 128, 32, 128], P('shot', 'slab'), may hold values from -6 to 6
- adjoint_current: bfloat16 [32, 128, 32, 128], P('shot', 'slab'), may hold values from -6 to 6
- velocity: float32 [128, 32, 128], P('slab'), may hold values from 1.5 to 4.2
- wavelet: float32 [32, 6], P('shot'), may hold values from -24 to 24
- source_cell: int32 [32], P('shot'), may hold values from 0 to 524287
- receiver_cell: int32 [32, 256], P('shot'), may hold values from 0 to 524287
- observed: float32 [32, 6, 256], P('shot'), may hold values from -6 to 6
- weight_in: bfloat16 [27, 2, 64], replicated, may hold values from -0.875 to 0.875
- bias_in: float32 [64], replicated, may hold values from -3 to 3
- weight_mid: bfloat16 [27, 64, 64], replicated, may hold values from -0.15625 to 0.15625
- bias_mid: float32 [64], replicated, may hold values from -3 to 3
- weight_out: bfloat16 [27, 64, 1], replicated, may hold values from -0.15625 to 0.15625
- bias_out: float32 [1], replicated, may hold values from -3 to 3
Outputs:
- velocity_next: float32 [128, 32, 128], P('slab')
- misfit: float32 [32, 6, 256], P('shot')
All inputs are finite; a program needn't handle non-finite values.
Results may differ from a plain program's by a relative error of at most 0.0023.
Values may be sent and summed in bfloat16 or wider, within the bound.
A program may use at most 64 MiB of HBM per device.

v0:
```python
import jax
import jax.numpy as jnp
from jax import lax
from jax.sharding import PartitionSpec as P

coeffs = (-205.0 / 72.0, 8.0 / 5.0, -1.0 / 5.0, 8.0 / 315.0, -1.0 / 560.0)
courant = 0.1
learn_rate = 0.2
center_speed = 3.0


def with_halo(block, sides, width):
    for axis, dim in sides:
        count = lax.axis_size(axis)
        forward = [(i, i + 1) for i in range(count - 1)]
        backward = [(target, source) for source, target in forward]
        low = lax.ppermute(
            lax.slice_in_dim(block, block.shape[dim] - width, None, axis=dim), axis, forward
        )
        high = lax.ppermute(lax.slice_in_dim(block, 0, width, axis=dim), axis, backward)
        block = jnp.concatenate([low, block, high], axis=dim)
    return block


def laplace(widened):
    count_rows = widened.shape[0] - 8
    middle = widened[4 : 4 + count_rows]
    width_y = middle.shape[1]
    width_z = middle.shape[2]
    padded = jnp.pad(middle, ((0, 0), (4, 4), (4, 4)))
    accumulated = 3.0 * coeffs[0] * middle
    for offset in range(1, 5):
        summed = (
            widened[4 + offset : 4 + offset + count_rows]
            + widened[4 - offset : 4 - offset + count_rows]
        )
        summed = (
            summed
            + padded[:, 4 + offset : 4 + offset + width_y, 4 : 4 + width_z]
            + padded[:, 4 - offset : 4 - offset + width_y, 4 : 4 + width_z]
        )
        summed = (
            summed
            + padded[:, 4 : 4 + width_y, 4 + offset : 4 + offset + width_z]
            + padded[:, 4 : 4 + width_y, 4 - offset : 4 - offset + width_z]
        )
        accumulated = accumulated + coeffs[offset] * summed
    return accumulated


def locate(wavefield, cell_index, first_row):
    plane_size = wavefield.shape[1] * wavefield.shape[2]
    slab_row = cell_index // plane_size
    inside = (slab_row >= first_row) & (slab_row < first_row + wavefield.shape[0])
    flat_index = jnp.where(inside, (slab_row - first_row) * plane_size + cell_index % plane_size, 0)
    return (inside, flat_index)


def inject(wavefield, cell_index, amounts, first_row):
    inside, flat_index = locate(wavefield, cell_index, first_row)
    values = jnp.where(inside, amounts, 0.0)
    return wavefield.reshape(-1).at[flat_index].add(values).reshape(wavefield.shape)


def record(wavefield, cell_index, first_row):
    inside, flat_index = locate(wavefield, cell_index, first_row)
    return jnp.where(inside, wavefield.reshape(-1)[flat_index], 0.0)


def advance(previous, current, kappa_block, laplacian, cell_index, amounts, first_row):
    stepped = 2.0 * current - previous + kappa_block * laplacian
    return inject(stepped, cell_index, amounts, first_row)


def widen(wavefield):
    return with_halo(wavefield, (("slab", 0),), 4)


def apply_taps(widened, kernel, shift):
    widened = jnp.pad(widened, ((0, 0), (0, 0), (0, 0), (1, 1)))
    depth_x = widened.shape[1] - 2
    depth_y = widened.shape[2] - 2
    depth_z = widened.shape[3] - 2
    accumulated = jnp.zeros((kernel.shape[2], depth_x, depth_y, depth_z), jnp.float32)
    for tap_index in range(27):
        offset_x = tap_index // 9
        offset_y = tap_index // 3 % 3
        offset_z = tap_index % 3
        window = widened[
            :,
            offset_x : offset_x + depth_x,
            offset_y : offset_y + depth_y,
            offset_z : offset_z + depth_z,
        ]
        accumulated = accumulated + jnp.einsum(
            "io,ixyz->oxyz", kernel[tap_index], window, preferred_element_type=jnp.float32
        )
    return accumulated + shift[:, None, None, None]


def convolve(features, kernel, shift):
    widened = with_halo(features, (("shot", 2), ("slab", 1)), 1)
    return apply_taps(widened, kernel, shift)


def shards(
    previous_field,
    current_field,
    adjoint_next,
    adjoint_current,
    velocity,
    wavelet,
    source_cell,
    receiver_cell,
    observed,
    weight_in,
    bias_in,
    weight_mid,
    bias_mid,
    weight_out,
    bias_out,
):
    slab_rows = velocity.shape[0]
    steps_total = wavelet.shape[1]
    first_row = lax.axis_index("slab") * slab_rows
    scaled = velocity * courant
    kappa = scaled * scaled
    receivers = receiver_cell[0]
    pulses = wavelet[0]
    previous = previous_field[0].astype(jnp.float32)
    current = current_field[0].astype(jnp.float32)
    snapshots = []
    traces = []
    for moment in range(steps_total):
        laplacian = laplace(widen(current))
        advanced = advance(
            previous, current, kappa, laplacian, source_cell, pulses[moment : moment + 1], first_row
        )
        snapshots.append(laplacian)
        traces.append(record(advanced, receivers, first_row))
        previous, current = (current, advanced)
    misfit = lax.psum(jnp.stack(traces), "slab") - observed[0]
    later = adjoint_next[0].astype(jnp.float32)
    adjoint_now = adjoint_current[0].astype(jnp.float32)
    imaging = jnp.zeros(velocity.shape, jnp.float32)
    for moment in reversed(range(steps_total)):
        laplacian = laplace(widen(adjoint_now))
        advanced = advance(
            later, adjoint_now, kappa, laplacian, receivers, misfit[moment], first_row
        )
        imaging = imaging + advanced * snapshots[moment]
        later, adjoint_now = (adjoint_now, advanced)
    shot_count = lax.axis_size("shot")
    share_rows = imaging.shape[1] // shot_count
    image_sum = lax.psum_scatter(imaging, "shot", scatter_dimension=1, tiled=True)
    mean_image = image_sum / shot_count
    update = learn_rate * mean_image
    y_start = lax.axis_index("shot") * share_rows
    velocity_rows = lax.dynamic_slice_in_dim(velocity, y_start, share_rows, 1)
    moved = velocity_rows - update
    features = jnp.stack([moved - center_speed, update]).astype(jnp.bfloat16)
    hidden_one = jnp.maximum(convolve(features, weight_in, bias_in), 0.0).astype(jnp.bfloat16)
    hidden_two = jnp.maximum(convolve(hidden_one, weight_mid, bias_mid), 0.0).astype(jnp.bfloat16)
    refined = moved + convolve(hidden_two, weight_out, bias_out)[0]
    gathered = lax.all_gather(refined, "shot", axis=1, tiled=True)
    return (gathered, misfit[None])


def solution(mesh):
    placed = (
        P("shot", "slab", None, None),
        P("shot", "slab", None, None),
        P("shot", "slab", None, None),
        P("shot", "slab", None, None),
        P("slab", None, None),
        P("shot", None),
        P("shot"),
        P("shot", None),
        P("shot", None, None),
        P(),
        P(),
        P(),
        P(),
        P(),
        P(),
    )
    return jax.shard_map(
        shards,
        mesh=mesh,
        in_specs=placed,
        out_specs=(P("slab", None, None), P("shot", None, None)),
        check_vma=False,
    )
```

profile of v0, /device:TPU:57, one launch (start us, length us, event | category | flops | bytes accessed | tf_op | source)
XLA Modules:
  0.0 691.3 jit_solution(13225365270769757046)
XLA Ops:
  8.2 3.0 collective-permute-start.2
  11.2 5.0 collective-permute-start.3
  22.1 2.8 fusion.677
  26.9 6.1 collective-permute-start.5
  34.6 2.8 fusion.678
  39.3 6.4 collective-permute-start.7
  47.7 6.1 collective-permute-start.1
  58.7 6.1 collective-permute-start.9
  71.0 6.4 collective-permute-start.11
  83.6 6.4 collective-permute-start.13
  99.4 2.8 fusion.682
  104.0 26.7 %psum.7 = f32[6,256]{1,0:T(8,128)S(1)} all-reduce(f32[6,256]{1,0:T(8,128)S(1)} %stack.24), channel_id=1, replica_groups=mesh['shot'=32,'slab'=16] {'slab'}, use_global_device_ids=true, to_apply=%region_0.1 | all-reduce | flops 1536 | bytes 12288 | tf_op jit(solution)/shard_map/psum | solution.py:142
  133.1 2.6 collective-permute-start.14
  135.8 5.6 collective-permute-start.15
  145.4 4.1 collective-permute-start.16
  149.5 4.2 collective-permute-start.17
  157.9 2.8 collective-permute-start.18
  160.7 5.5 collective-permute-start.19
  172.2 6.4 collective-permute-start.21
  184.5 6.4 collective-permute-start.23
  197.2 342.5 %all-reduce.18.cloned.1.call-done = f32[8,32,128]{2,0,1:T(8,128)} async-done(((f32[8,32,128]{2,0,1:T(8,128)}), f32[8,32,128]{2,0,1:T(8,128)}) %all-reduce.18.cloned.1.call-update) | async-done | bytes 131088
  543.0 4.5 collective-permute-start.25
  548.3 3.4 collective-permute-start.26
  553.6 5.1 collective-permute-done.27
  565.2 2.8 collective-permute-start.28
  568.0 10.9 %collective-permute-start.29 = (bf16[64,8,1,128]{3,0,1,2:T(8,128)(2,1)S(1)}, bf16[64,8,1,128]{3,0,1,2:T(8,128)(2,1)S(1)}, u32[]{:S(2)}, u32[]{:S(2)}) collective-permute-start(bf16[64,8,1,128]{3,0,1,2:T(8,128)(2,1)S(1)} %bitcast.937), channel_id=1, source_target_pairs={{16,0},{32,16},{48,32},{64,48},{80,64},{96,80},{112,96},{128,112},... | collective-permute-start | bytes 393224 | tf_op jit(solution)/shard_map/ppermute | solution.py:20
  581.8 3.4 collective-permute-start.31
  586.4 2.9 collective-permute-done.31
  598.3 12.3 %collective-permute-start.33 = (bf16[64,8,1,128]{3,0,1,2:T(8,128)(2,1)S(1)}, bf16[64,8,1,128]{3,0,1,2:T(8,128)(2,1)S(1)}, u32[]{:S(2)}, u32[]{:S(2)}) collective-permute-start(bf16[64,8,1,128]{3,0,1,2:T(8,128)(2,1)S(1)} %bitcast.950), channel_id=1, source_target_pairs={{16,0},{32,16},{48,32},{64,48},{80,64},{96,80},{112,96},{128,112},... | collective-permute-start | bytes 393224 | tf_op jit(solution)/shard_map/ppermute | solution.py:20
  613.6 3.4 collective-permute-start.35
  617.2 3.9 collective-permute-done.35
  627.1 56.7 %all_gather.3 = f32[8,32,128]{2,0,1:T(8,128)S(1)} all-gather(f32[8,1,128]{2,0,1:T(8,128)S(1)} %bitcast_add_fusion), channel_id=1, replica_groups=mesh['shot'=32,'slab'=16] {'shot'}, dimensions={1}, use_global_device_ids=true | all-gather | bytes 135168 | tf_op jit(solution)/shard_map/all_gather | solution.py:165
  (222 shorter events, 103.1 us)
Async XLA Ops:
  7.2 532.5 %all-reduce.18.cloned.1.call-start = ((), (), s32[]{:S(2)}) async-start(), calls=%async_computation | async-start | bytes 262144
  8.2 12.6 %collective-permute-start.2 = (f32[4,32,128]{2,1,0:T(8,128)S(1)}, f32[4,32,128]{2,1,0:T(8,128)S(1)}, u32[]{:S(2)}, u32[]{:S(2)}) collective-permute-start(f32[4,32,128]{2,1,0:T(8,128)S(1)} %get-tuple-element.127), channel_id=1, source_target_pairs={{1,0},{2,1},{3,2},{4,3},{5,4},{6,5},{7,6},{8,7},{9,8},{10,9},{11,1... | collective-permute-start | bytes 196616 | tf_op jit(solution)/shard_map/ppermute | solution.py:20
  11.2 9.7 %collective-permute-start.3 = (f32[4,32,128]{2,1,0:T(8,128)S(1)}, f32[4,32,128]{2,1,0:T(8,128)S(1)}, u32[]{:S(2)}, u32[]{:S(2)}) collective-permute-start(f32[4,32,128]{2,1,0:T(8,128)S(1)} %get-tuple-element.128), channel_id=1, source_target_pairs={{0,1},{1,2},{2,3},{3,4},{4,5},{5,6},{6,7},{7,8},{8,9},{9,10},{10,1... | collective-permute-start | bytes 196616 | tf_op jit(solution)/shard_map/ppermute | solution.py:17
  24.9 8.0 %collective-permute-start.4 = (f32[4,32,128]{2,1,0:T(8,128)S(1)}, f32[4,32,128]{2,1,0:T(8,128)S(1)}, u32[]{:S(2)}, u32[]{:S(2)}) collective-permute-start(f32[4,32,128]{2,1,0:T(8,128)S(1)} %bitcast.973), channel_id=1, source_target_pairs={{1,0},{2,1},{3,2},{4,3},{5,4},{6,5},{7,6},{8,7},{9,8},{10,9},{11,1... | collective-permute-start | bytes 196616 | tf_op jit(solution)/shard_map/ppermute | solution.py:20
  26.9 7.4 %collective-permute-start.5 = (f32[4,32,128]{2,1,0:T(8,128)S(1)}, f32[4,32,128]{2,1,0:T(8,128)S(1)}, u32[]{:S(2)}, u32[]{:S(2)}) collective-permute-start(f32[4,32,128]{2,1,0:T(8,128)S(1)} %bitcast.970), channel_id=1, source_target_pairs={{0,1},{1,2},{2,3},{3,4},{4,5},{5,6},{6,7},{7,8},{8,9},{9,10},{10,1... | collective-permute-start | bytes 196616 | tf_op jit(solution)/shard_map/ppermute | solution.py:17
  37.4 16.3 %collective-permute-start.6 = (f32[4,32,128]{2,1,0:T(8,128)S(1)}, f32[4,32,128]{2,1,0:T(8,128)S(1)}, u32[]{:S(2)}, u32[]{:S(2)}) collective-permute-start(f32[4,32,128]{2,1,0:T(8,128)S(1)} %bitcast.969), channel_id=1, source_target_pairs={{1,0},{2,1},{3,2},{4,3},{5,4},{6,5},{7,6},{8,7},{9,8},{10,9},{11,1... | collective-permute-start | bytes 196616 | tf_op jit(solution)/shard_map/ppermute | solution.py:20
  39.3 14.4 %collective-permute-start.7 = (f32[4,32,128]{2,1,0:T(8,128)S(1)}, f32[4,32,128]{2,1,0:T(8,128)S(1)}, u32[]{:S(2)}, u32[]{:S(2)}) collective-permute-start(f32[4,32,128]{2,1,0:T(8,128)S(1)} %bitcast.968), channel_id=1, source_target_pairs={{0,1},{1,2},{2,3},{3,4},{4,5},{5,6},{6,7},{7,8},{8,9},{9,10},{10,1... | collective-permute-start | bytes 196616 | tf_op jit(solution)/shard_map/ppermute | solution.py:17
  45.7 44.3 %collective-permute-start = (f32[4,32,128]{2,1,0:T(8,128)S(1)}, f32[4,32,128]{2,1,0:T(8,128)S(1)}, u32[]{:S(2)}, u32[]{:S(2)}) collective-permute-start(f32[4,32,128]{2,1,0:T(8,128)S(1)} %get-tuple-element.129), channel_id=1, source_target_pairs={{1,0},{2,1},{3,2},{4,3},{5,4},{6,5},{7,6},{8,7},{9,8},{10,9},{11,1... | collective-permute-start | bytes 196616 | tf_op jit(solution)/shard_map/ppermute | solution.py:20
  47.7 42.4 %collective-permute-start.1 = (f32[4,32,128]{2,1,0:T(8,128)S(1)}, f32[4,32,128]{2,1,0:T(8,128)S(1)}, u32[]{:S(2)}, u32[]{:S(2)}) collective-permute-start(f32[4,32,128]{2,1,0:T(8,128)S(1)} %get-tuple-element.130), channel_id=1, source_target_pairs={{0,1},{1,2},{2,3},{3,4},{4,5},{5,6},{6,7},{7,8},{8,9},{9,10},{10,1... | collective-permute-start | bytes 196616 | tf_op jit(solution)/shard_map/ppermute | solution.py:17
  56.8 8.0 %collective-permute-start.8 = (f32[4,32,128]{2,1,0:T(8,128)S(1)}, f32[4,32,128]{2,1,0:T(8,128)S(1)}, u32[]{:S(2)}, u32[]{:S(2)}) collective-permute-start(f32[4,32,128]{2,1,0:T(8,128)S(1)} %bitcast.979), channel_id=1, source_target_pairs={{1,0},{2,1},{3,2},{4,3},{5,4},{6,5},{7,6},{8,7},{9,8},{10,9},{11,1... | collective-permute-start | bytes 196616 | tf_op jit(solution)/shard_map/ppermute | solution.py:20
  58.7 7.4 %collective-permute-start.9 = (f32[4,32,128]{2,1,0:T(8,128)S(1)}, f32[4,32,128]{2,1,0:T(8,128)S(1)}, u32[]{:S(2)}, u32[]{:S(2)}) collective-permute-start(f32[4,32,128]{2,1,0:T(8,128)S(1)} %bitcast.971), channel_id=1, source_target_pairs={{0,1},{1,2},{2,3},{3,4},{4,5},{5,6},{6,7},{7,8},{8,9},{9,10},{10,1... | collective-permute-start | bytes 196616 | tf_op jit(solution)/shard_map/ppermute | solution.py:17
  69.1 8.3 %collective-permute-start.10 = (f32[4,32,128]{2,1,0:T(8,128)S(1)}, f32[4,32,128]{2,1,0:T(8,128)S(1)}, u32[]{:S(2)}, u32[]{:S(2)}) collective-permute-start(f32[4,32,128]{2,1,0:T(8,128)S(1)} %bitcast.980), channel_id=1, source_target_pairs={{1,0},{2,1},{3,2},{4,3},{5,4},{6,5},{7,6},{8,7},{9,8},{10,9},{11,1... | collective-permute-start | bytes 196616 | tf_op jit(solution)/shard_map/ppermute | solution.py:20
  71.0 7.7 %collective-permute-start.11 = (f32[4,32,128]{2,1,0:T(8,128)S(1)}, f32[4,32,128]{2,1,0:T(8,128)S(1)}, u32[]{:S(2)}, u32[]{:S(2)}) collective-permute-start(f32[4,32,128]{2,1,0:T(8,128)S(1)} %bitcast.972), channel_id=1, source_target_pairs={{0,1},{1,2},{2,3},{3,4},{4,5},{5,6},{6,7},{7,8},{8,9},{9,10},{10,1... | collective-permute-start | bytes 196616 | tf_op jit(solution)/shard_map/ppermute | solution.py:17
  81.7 17.4 %collective-permute-start.12 = (f32[4,32,128]{2,1,0:T(8,128)S(1)}, f32[4,32,128]{2,1,0:T(8,128)S(1)}, u32[]{:S(2)}, u32[]{:S(2)}) collective-permute-start(f32[4,32,128]{2,1,0:T(8,128)S(1)} %bitcast.967), channel_id=1, source_target_pairs={{1,0},{2,1},{3,2},{4,3},{5,4},{6,5},{7,6},{8,7},{9,8},{10,9},{11,1... | collective-permute-start | bytes 196616 | tf_op jit(solution)/shard_map/ppermute | solution.py:20
  83.6 15.5 %collective-permute-start.13 = (f32[4,32,128]{2,1,0:T(8,128)S(1)}, f32[4,32,128]{2,1,0:T(8,128)S(1)}, u32[]{:S(2)}, u32[]{:S(2)}) collective-permute-start(f32[4,32,128]{2,1,0:T(8,128)S(1)} %bitcast.966), channel_id=1, source_target_pairs={{0,1},{1,2},{2,3},{3,4},{4,5},{5,6},{6,7},{7,8},{8,9},{9,10},{10,1... | collective-permute-start | bytes 196616 | tf_op jit(solution)/shard_map/ppermute | solution.py:17
  133.1 8.3 %collective-permute-start.14 = (f32[4,32,128]{2,1,0:T(8,128)S(1)}, f32[4,32,128]{2,1,0:T(8,128)S(1)}, u32[]{:S(2)}, u32[]{:S(2)}) collective-permute-start(f32[4,32,128]{2,1,0:T(8,128)S(1)} %bitcast.981), channel_id=1, source_target_pairs={{1,0},{2,1},{3,2},{4,3},{5,4},{6,5},{7,6},{8,7},{9,8},{10,9},{11,1... | collective-permute-start | bytes 196616 | tf_op jit(solution)/shard_map/ppermute | solution.py:20
  135.8 6.9 %collective-permute-start.15 = (f32[4,32,128]{2,1,0:T(8,128)S(1)}, f32[4,32,128]{2,1,0:T(8,128)S(1)}, u32[]{:S(2)}, u32[]{:S(2)}) collective-permute-start(f32[4,32,128]{2,1,0:T(8,128)S(1)} %bitcast.974), channel_id=1, source_target_pairs={{0,1},{1,2},{2,3},{3,4},{4,5},{5,6},{6,7},{7,8},{8,9},{9,10},{10,1... | collective-permute-start | bytes 196616 | tf_op jit(solution)/shard_map/ppermute | solution.py:17
  145.4 8.3 %collective-permute-start.16 = (f32[4,32,128]{2,1,0:T(8,128)S(1)}, f32[4,32,128]{2,1,0:T(8,128)S(1)}, u32[]{:S(2)}, u32[]{:S(2)}) collective-permute-start(f32[4,32,128]{2,1,0:T(8,128)S(1)} %bitcast.982), channel_id=1, source_target_pairs={{1,0},{2,1},{3,2},{4,3},{5,4},{6,5},{7,6},{8,7},{9,8},{10,9},{11,1... | collective-permute-start | bytes 196616 | tf_op jit(solution)/shard_map/ppermute | solution.py:20
  157.9 8.4 %collective-permute-start.18 = (f32[4,32,128]{2,1,0:T(8,128)S(1)}, f32[4,32,128]{2,1,0:T(8,128)S(1)}, u32[]{:S(2)}, u32[]{:S(2)}) collective-permute-start(f32[4,32,128]{2,1,0:T(8,128)S(1)} %bitcast.983), channel_id=1, source_target_pairs={{1,0},{2,1},{3,2},{4,3},{5,4},{6,5},{7,6},{8,7},{9,8},{10,9},{11,1... | collective-permute-start | bytes 196616 | tf_op jit(solution)/shard_map/ppermute | solution.py:20
  160.7 6.8 collective-permute-start.19
  170.3 8.3 %collective-permute-start.20 = (f32[4,32,128]{2,1,0:T(8,128)S(1)}, f32[4,32,128]{2,1,0:T(8,128)S(1)}, u32[]{:S(2)}, u32[]{:S(2)}) collective-permute-start(f32[4,32,128]{2,1,0:T(8,128)S(1)} %bitcast.984), channel_id=1, source_target_pairs={{1,0},{2,1},{3,2},{4,3},{5,4},{6,5},{7,6},{8,7},{9,8},{10,9},{11,1... | collective-permute-start | bytes 196616 | tf_op jit(solution)/shard_map/ppermute | solution.py:20
  172.2 7.7 %collective-permute-start.21 = (f32[4,32,128]{2,1,0:T(8,128)S(1)}, f32[4,32,128]{2,1,0:T(8,128)S(1)}, u32[]{:S(2)}, u32[]{:S(2)}) collective-permute-start(f32[4,32,128]{2,1,0:T(8,128)S(1)} %bitcast.977), channel_id=1, source_target_pairs={{0,1},{1,2},{2,3},{3,4},{4,5},{5,6},{6,7},{7,8},{8,9},{9,10},{10,1... | collective-permute-start | bytes 196616 | tf_op jit(solution)/shard_map/ppermute | solution.py:17
  182.6 8.3 %collective-permute-start.22 = (f32[4,32,128]{2,1,0:T(8,128)S(1)}, f32[4,32,128]{2,1,0:T(8,128)S(1)}, u32[]{:S(2)}, u32[]{:S(2)}) collective-permute-start(f32[4,32,128]{2,1,0:T(8,128)S(1)} %bitcast.985), channel_id=1, source_target_pairs={{1,0},{2,1},{3,2},{4,3},{5,4},{6,5},{7,6},{8,7},{9,8},{10,9},{11,1... | collective-permute-start | bytes 196616 | tf_op jit(solution)/shard_map/ppermute | solution.py:20
  184.5 7.7 %collective-permute-start.23 = (f32[4,32,128]{2,1,0:T(8,128)S(1)}, f32[4,32,128]{2,1,0:T(8,128)S(1)}, u32[]{:S(2)}, u32[]{:S(2)}) collective-permute-start(f32[4,32,128]{2,1,0:T(8,128)S(1)} %bitcast.978), channel_id=1, source_target_pairs={{0,1},{1,2},{2,3},{3,4},{4,5},{5,6},{6,7},{7,8},{8,9},{9,10},{10,1... | collective-permute-start | bytes 196616 | tf_op jit(solution)/shard_map/ppermute | solution.py:17
  551.7 7.0 %collective-permute-start.27 = (bf16[2,1,3,128]{3,0,1,2:T(2,128)(2,1)S(1)}, bf16[2,1,3,128]{3,0,1,2:T(2,128)(2,1)S(1)}, u32[]{:S(2)}, u32[]{:S(2)}) collective-permute-start(bf16[2,1,3,128]{3,0,1,2:T(2,128)(2,1)S(1)} %get-tuple-element.136), channel_id=1, source_target_pairs={{1,0},{2,1},{3,2},{4,3},{5,4},{6,5},{7,6},{8,7},{9,8},{10,9},{11,1... | collective-permute-start | bytes 4616 | tf_op jit(solution)/shard_map/ppermute | solution.py:20
  565.2 13.7 %collective-permute-start.28 = (bf16[64,8,1,128]{3,0,1,2:T(8,128)(2,1)S(1)}, bf16[64,8,1,128]{3,0,1,2:T(8,128)(2,1)S(1)}, u32[]{:S(2)}, u32[]{:S(2)}) collective-permute-start(bf16[64,8,1,128]{3,0,1,2:T(8,128)(2,1)S(1)} %bitcast.936), channel_id=1, source_target_pairs={{0,16},{16,32},{32,48},{48,64},{64,80},{80,96},{96,112},{112,128},... | collective-permute-start | bytes 393224 | tf_op jit(solution)/shard_map/ppermute | solution.py:17
  568.0 11.8 %collective-permute-start.29 = (bf16[64,8,1,128]{3,0,1,2:T(8,128)(2,1)S(1)}, bf16[64,8,1,128]{3,0,1,2:T(8,128)(2,1)S(1)}, u32[]{:S(2)}, u32[]{:S(2)}) collective-permute-start(bf16[64,8,1,128]{3,0,1,2:T(8,128)(2,1)S(1)} %bitcast.937), channel_id=1, source_target_pairs={{16,0},{32,16},{48,32},{64,48},{80,64},{96,80},{112,96},{128,112},... | collective-permute-start | bytes 393224 | tf_op jit(solution)/shard_map/ppermute | solution.py:20
  579.9 6.5 collective-permute-start.30
  581.8 7.5 %collective-permute-start.31 = (bf16[64,1,3,128]{3,0,1,2:T(8,128)(2,1)S(1)}, bf16[64,1,3,128]{3,0,1,2:T(8,128)(2,1)S(1)}, u32[]{:S(2)}, u32[]{:S(2)}) collective-permute-start(bf16[64,1,3,128]{3,0,1,2:T(8,128)(2,1)S(1)} %get-tuple-element.103), channel_id=1, source_target_pairs={{1,0},{2,1},{3,2},{4,3},{5,4},{6,5},{7,6},{8,7},{9,8},{10,9},{11,1... | collective-permute-start | bytes 147464 | tf_op jit(solution)/shard_map/ppermute | solution.py:20
  596.4 14.4 %collective-permute-start.32 = (bf16[64,8,1,128]{3,0,1,2:T(8,128)(2,1)S(1)}, bf16[64,8,1,128]{3,0,1,2:T(8,128)(2,1)S(1)}, u32[]{:S(2)}, u32[]{:S(2)}) collective-permute-start(bf16[64,8,1,128]{3,0,1,2:T(8,128)(2,1)S(1)} %bitcast.949), channel_id=1, source_target_pairs={{0,16},{16,32},{32,48},{48,64},{64,80},{80,96},{96,112},{112,128},... | collective-permute-start | bytes 393224 | tf_op jit(solution)/shard_map/ppermute | solution.py:17
  598.3 13.3 %collective-permute-start.33 = (bf16[64,8,1,128]{3,0,1,2:T(8,128)(2,1)S(1)}, bf16[64,8,1,128]{3,0,1,2:T(8,128)(2,1)S(1)}, u32[]{:S(2)}, u32[]{:S(2)}) collective-permute-start(bf16[64,8,1,128]{3,0,1,2:T(8,128)(2,1)S(1)} %bitcast.950), channel_id=1, source_target_pairs={{16,0},{32,16},{48,32},{64,48},{80,64},{96,80},{112,96},{128,112},... | collective-permute-start | bytes 393224 | tf_op jit(solution)/shard_map/ppermute | solution.py:20
  613.6 7.5 %collective-permute-start.35 = (bf16[64,1,3,128]{3,0,1,2:T(8,128)(2,1)S(1)}, bf16[64,1,3,128]{3,0,1,2:T(8,128)(2,1)S(1)}, u32[]{:S(2)}, u32[]{:S(2)}) collective-permute-start(bf16[64,1,3,128]{3,0,1,2:T(8,128)(2,1)S(1)} %get-tuple-element.101), channel_id=1, source_target_pairs={{1,0},{2,1},{3,2},{4,3},{5,4},{6,5},{7,6},{8,7},{9,8},{10,9},{11,1... | collective-permute-start | bytes 147464 | tf_op jit(solution)/shard_map/ppermute | solution.py:20
  (16 other events, 599.1 us)
Sparse Core Ops, SparseCore 0:
  196.0 343.6 all-reduce.17
where the time goes:
time: 693 us; the launch traced here: 691 us
  waiting for transfers between devices  367 us (53%)
  starting transfers between devices  149 us (22%)
  blocking collectives  83.4 us (12%)
  other arithmetic  41.2 us (6%)
  between operations  18.5 us (3%)
  matrix products  16.6 us (2%)
  local copies, waits for them, and re-layouts  15.7 us (2%)
    unnamed x2, waiting for transfers between devices  343 us
    ppermute x18, starting transfers between devices, with_halo(): lax.ppermute(lax.slice_in_dim(block, block.shape[dim] - width, None, axis...  84.3 us
    ppermute x18, starting transfers between devices, with_halo(): lax.ppermute(lax.slice_in_dim(block, 0, width, axis=dim), axis, backward)  64.3 us
    all_gather x1, blocking collectives, shards(): gathered = lax.all_gather(refined, 'shot', axis=1, tiled=True)  56.7 us
    scatter-add x12, other arithmetic, inject(): wavefield.reshape(-1).at[flat_index].add(values).reshape(wavefield.shape)  30.4 us
    psum x1, blocking collectives, shards(): misfit = lax.psum(jnp.stack(traces), 'slab') - observed[0]  26.7 us
    dot_general x81, matrix products, apply_taps(): jnp.einsum('io,ixyz->oxyz', kernel[tap_index], window, preferred_element_...  16.6 us
    ppermute x18, waiting for transfers between devices, with_halo(): lax.ppermute(lax.slice_in_dim(block, 0, width, axis=dim), axis, backward)  14.5 us
  transfers between devices with their start and end apart: 37, of which 15 were waited for; matrix products, arithmetic and copies ran while one was open for 3% of the time, Pallas kernels for 0%

commit v1 on v0

v1 whole, which is shorter than its diff:
```python
import functools

import jax
import jax.numpy as jnp
from jax import lax
from jax.experimental import pallas as pl
from jax.experimental.pallas import tpu as pltpu
from jax.sharding import PartitionSpec as P

COEFFS = (-205.0 / 72.0, 8.0 / 5.0, -1.0 / 5.0, 8.0 / 315.0, -1.0 / 560.0)
COURANT = 0.1
RATE = 0.2
CENTER = 3.0
MID = 2.75
MESH = pl.DeviceIdType.MESH
F32 = jnp.float32
BF16 = jnp.bfloat16
NT = (((1,), (1,)), ((), ()))
STEPS = 6
TOP, ROWS = 8, 32
YS = slice(TOP, TOP + ROWS)


def dot(a, b):
    return jnp.dot(a, b, preferred_element_type=F32)


def split(x, pieces):
    parts = []
    for _ in range(pieces):
        part = x.astype(BF16)
        parts.append(part)
        x = x - part.astype(F32)
    return parts


def z_combine(g, lane):
    low = jnp.where(lane == 0, 0.0, pltpu.roll(g[0:64], 1, 1))
    high = jnp.where(lane == 127, 0.0, pltpu.roll(g[128:192], 127, 1))
    return g[64:128] + low + high


def kernel(
    slabs, shots,
    prev, cur, anext, acur, vel, wav, src, rec, obs, w1, b1, wm, b2, w3, b3,
    out, mis,
    u0, u1, wa0, wa1, da, db, zs, js, kap, lap, hom, img, imgt,
    sv, rv, rc, rp, sb, rb, tr, rt, mf, hot, pick, lane_hot, src_hot, bands, bandl,
    ri, fs, rf, feat, g1, h1, h2, row, ro,
    init_s, init_r, round_s, round_r, tr_s, tr_r, im_s, im_r, ft_s, ft_r, ou_s, ou_r,
):
    s = lax.axis_index("shot")
    b = lax.axis_index("slab")

    def shot_at(k):
        return lax.rem(s + k + shots, shots)

    def slab_at(k):
        return lax.rem(b + k + slabs, slabs)

    def inside(k):
        return jnp.where((b + k >= 0) & (b + k < slabs), 1.0, 0.0).astype(F32)

    def send(source, target, ss, rs, shot, slab):
        copy = pltpu.make_async_remote_copy(
            src_ref=source, dst_ref=target, send_sem=ss, recv_sem=rs,
            device_id=(shot, slab), device_id_type=MESH)
        copy.start()
        return copy

    barrier = pltpu.get_barrier_semaphore()
    peers = [(s, slab_at(k)) for k in range(1, slabs)]
    peers += [(shot_at(k), b) for k in range(1, shots)]
    cross = [(dx, dy) for dy in range(-3, 4) for dx in (-1, 0, 1) if (dx, dy) != (0, 0)]
    peers += [(shot_at(dy), slab_at(dx)) for dx, dy in cross if dx != 0 and dy != 0]
    for peer in peers:
        pl.semaphore_signal(barrier, inc=1, device_id=peer, device_id_type=MESH)

    sv[...] = (vel[...] - MID).astype(BF16)
    pl.semaphore_wait(barrier, len(peers))

    sent = []
    first = []
    for side, step in ((0, 1), (1, -1)):
        target = slab_at(step)
        edge = pl.ds(4, 4) if step == 1 else pl.ds(0, 4)
        for f, (now, old) in enumerate(((cur, prev), (acur, anext))):
            first.append(send(now.at[0], rc.at[side, f], init_s.at[side, 2 * f], init_r.at[side, 2 * f], s, target))
            first.append(send(old.at[0, edge], rp.at[side, f], init_s.at[side, 2 * f + 1], init_r.at[side, 2 * f + 1], s, target))
        first.append(send(sv, rv.at[1 + side], init_s.at[side, 4], init_r.at[side, 4], s, target))
    far = []
    for side, step in ((0, 2), (1, -2)):
        far.append(send(sv, rv.at[3 * side], init_s.at[side, 5], init_r.at[side, 5], s, slab_at(step)))
    sent += first + far

    lane = lax.broadcasted_iota(jnp.int32, (64, 128), 1)
    diff = jnp.abs(lax.broadcasted_iota(jnp.int32, (128, 128), 0) - lax.broadcasted_iota(jnp.int32, (128, 128), 1))
    band = jnp.where(diff == 0, 3.0 * COEFFS[0], 0.0)
    for m in range(1, 5):
        band = jnp.where(diff == m, COEFFS[m], band)
    band_h, band_l = split(band, 2)
    bands[0:128, :] = band_h
    bands[128:256, :] = band_h
    bandl[...] = band_l

    for ref in (u0, u1, wa0, wa1, da, db):
        ref[:, 0:TOP, :] = jnp.zeros((ref.shape[0], TOP, 128), F32)
        ref[:, TOP + ROWS:, :] = jnp.zeros((ref.shape[0], 8, 128), F32)
    db[:, YS, :] = jnp.zeros((db.shape[0], ROWS, 128), F32)
    u0[8:16, YS, :] = cur[0].astype(F32)
    u1[8:16, YS, :] = acur[0].astype(F32)
    wa0[8:16, YS, :] = prev[0].astype(F32)
    wa1[8:16, YS, :] = anext[0].astype(F32)
    scaled = vel[...] * COURANT
    kap[16:24] = scaled * scaled

    cells = rec[...]
    rec_row = lax.shift_right_logical(cells, 7)
    rec_lane = cells & 127
    sub = lax.broadcasted_iota(jnp.int32, (8, 256), 0)
    digits = jnp.where(sub == 0, lax.shift_right_logical(rec_row, 6),
                       jnp.where(sub == 1, rec_row & 63, jnp.where(sub == 2, rec_lane, 0)))
    eye = jnp.where(
        lax.broadcasted_iota(jnp.int32, (256, 256), 0) == lax.broadcasted_iota(jnp.int32, (256, 256), 1),
        1.0, 0.0).astype(BF16)
    columns = lax.dot_general(eye, digits.astype(F32).astype(BF16), NT, preferred_element_type=F32)
    row_col = columns[:, 0:1] * 64.0 + columns[:, 1:2] - (b * 256).astype(F32)
    lane_col = columns[:, 2:3]
    lane_hot[...] = jnp.where(lane_col == lax.broadcasted_iota(jnp.int32, (256, 128), 1).astype(F32), 1.0, 0.0)
    pick[...] = jnp.where(
        row_col == lax.broadcasted_iota(jnp.int32, (256, 256), 1).astype(F32), 1.0, 0.0).astype(BF16)
    relative = rec_row - (b * 256 - 20 * ROWS)
    for q in range(6):
        hot[256 * q:256 * q + 256, :] = jnp.where(
            lax.broadcasted_iota(jnp.int32, (256, 256), 0) + 256 * q == relative, 1.0, 0.0).astype(BF16)
    cell = src[0]
    src_plane = lax.shift_right_logical(cell, 12)
    src_row = lax.shift_right_logical(cell, 7) & 31
    src_lane = cell & 127
    src_hot[...] = jnp.where(
        (lax.broadcasted_iota(jnp.int32, (ROWS, 128), 0) == src_row)
        & (lax.broadcasted_iota(jnp.int32, (ROWS, 128), 1) == src_lane), 1.0, 0.0)

    def z_pass(field, lo, n):
        for c in range(n // 8):
            x = field[lo + 8 * c:lo + 8 * c + 8, YS, :].reshape(256, 128)
            hi, low = split(x, 2)
            z = dot(jnp.concatenate([hi, low], axis=1), bands[...]) + dot(hi, bandl[...])
            zs[8 * c:8 * c + 8] = z.reshape(8, ROWS, 128)

    def advance(field, old, lo, n, kap_lo, extra):
        def one(i, carry):
            j = lo + i
            here = field[j, YS, :]
            acc = zs[i]
            for m in range(1, 5):
                around = (field[j + m, YS, :] + field[j - m, YS, :]) + (
                    field[j, TOP + m:TOP + m + ROWS, :] + field[j, TOP - m:TOP - m + ROWS, :])
                acc = acc + COEFFS[m] * around
            new = 2.0 * here - old[j, YS, :] + kap[kap_lo + i] * acc
            old[j, YS, :] = extra(i, j, new, acc)
            return carry
        lax.fori_loop(0, n, one, 0, unroll=2)

    def plain(i, j, new, acc):
        return new

    def forward_extra(n, keep_lo):
        weight = wav[0, n]
        first_plane = b * 8 - 8

        def extra(i, j, new, acc):
            zs[i] = acc
            amount = jnp.where(src_plane == first_plane + j, weight, 0.0)
            return new + src_hot[...] * amount
        return extra

    def sample(field, n):
        x = field[8:16, YS, :].reshape(256, 128)
        g = dot(pick[...], jnp.concatenate(split(x, 3), axis=1))
        hot3 = jnp.concatenate([lane_hot[...]] * 3, axis=1)
        values = lax.dot_general(jnp.ones((8, 384), BF16), (g * hot3).astype(BF16), NT, preferred_element_type=F32)
        tr[n:n + 1, :] = values[0:1, :]

    tr[...] = jnp.zeros((8, 256), F32)
    left, right = inside(-1), inside(1)
    for copy in first:
        copy.wait_recv()
    for f, (now, old) in enumerate(((u0, wa0), (u1, wa1))):
        now[0:8, YS, :] = rc[0, f].astype(F32) * left
        now[16:24, YS, :] = rc[1, f].astype(F32) * right
        old[4:8, YS, :] = rp[0, f].astype(F32) * left
        old[16:20, YS, :] = rp[1, f].astype(F32) * right

    def kappa_of(slot, valid):
        value = (rv[slot].astype(F32) + MID) * COURANT
        return value * value * valid

    kap[8:16] = kappa_of(1, left)
    kap[24:32] = kappa_of(2, right)

    for r in range(3):
        n = 2 * r
        z_pass(u0, 4, 16)
        advance(u0, wa0, 4, 16, 12, forward_extra(n, 4))
        lap[n] = zs[4:12]
        z_pass(wa0, 8, 8)
        advance(wa0, u0, 8, 8, 16, forward_extra(n + 1, 0))
        lap[n + 1] = zs[0:8]
        z_pass(u1, 4, 16)
        advance(u1, wa1, 4, 16, 12, plain)
        z_pass(wa1, 8, 8)
        advance(wa1, u1, 8, 8, 16, plain)
        if r < 2:
            sb[r, 0] = u0[8:16, YS, :].astype(BF16)
            sb[r, 1] = u1[8:16, YS, :].astype(BF16)
            copies = [
                send(sb.at[r], rb.at[r, side], round_s.at[r, side], round_r.at[r, side], s, slab_at(step))
                for side, step in ((0, 1), (1, -1))]
            sent += copies
        sample(wa0, n)
        sample(u0, n + 1)
        hom[STEPS - 1 - n] = wa1[8:16, YS, :]
        hom[STEPS - 2 - n] = u1[8:16, YS, :]
        if r < 2:
            for copy in copies:
                copy.wait_recv()
            for f, now in enumerate((u0, u1)):
                now[0:8, YS, :] = rb[r, 0, f].astype(F32) * left
                now[16:24, YS, :] = rb[r, 1, f].astype(F32) * right

    for k in range(1, slabs):
        send(tr, rt.at[k - 1], tr_s, tr_r, s, slab_at(k))
    image = hom[0] * lap[0]
    for n in range(1, STEPS):
        image = image + hom[n] * lap[n]
    img[...] = image
    for copy in far:
        copy.wait_recv()
    kap[0:8] = kappa_of(0, inside(-2))
    kap[32:40] = kappa_of(3, inside(2))
    pltpu.make_async_copy(rt, rt, tr_r).wait()
    total = tr[...]
    for k in range(slabs - 1):
        total = total + rt[k]
    traces = total[0:STEPS] - obs[0]
    mis[0] = traces
    mf[...] = jnp.zeros((8, 256), F32)
    mf[0:STEPS, :] = traces
    amounts = jnp.zeros((256, 8), F32)
    for part in split(mf[...], 3):
        amounts = amounts + lax.dot_general(eye, part, NT, preferred_element_type=F32)

    def inject(n, plane, planes):
        parts = split(amounts[:, n:n + 1] * lane_hot[...], 2)
        rhs = jnp.concatenate(parts, axis=1)
        for c in range(planes // 8):
            start = (plane + 8 * c) * ROWS
            both = dot(hot[start:start + 256, :], rhs)
            yield c, (both[:, 0:128] + both[:, 128:256]).reshape(8, ROWS, 128)

    for c, values in inject(5, 0, 48):
        da[8 * c:8 * c + 8, YS, :] = values
    img[...] += da[20:28, YS, :] * lap[5]

    def with_misfit(i, j, new, acc):
        return new + js[i]

    near, old = da, db
    for n in range(4, -1, -1):
        reach = 4 * n
        lo, planes = 20 - reach, 8 + 2 * reach
        z_pass(near, lo, planes)
        for c, values in inject(n, lo, planes):
            js[8 * c:8 * c + 8] = values
        advance(near, old, lo, planes, lo - 4, with_misfit)
        near, old = old, near
        img[...] += near[20:28, YS, :] * lap[n]

    imgt[...] = jnp.swapaxes(img[...], 0, 1)
    for k in range(1, shots):
        send(imgt.at[shot_at(k)], ri.at[k - 1], im_s, im_r, shot_at(k), b)
    mine = lax.broadcasted_iota(jnp.int32, (8, ROWS, 128), 1) == s
    own_velocity = jnp.sum(jnp.where(mine, vel[...], 0.0), axis=1)
    pltpu.make_async_copy(ri, ri, im_r).wait()
    summed = imgt[s]
    for k in range(shots - 1):
        summed = summed + ri[k]
    update = RATE * (summed / shots)
    moved = own_velocity - update
    fs[0:8, :] = (moved - CENTER).astype(BF16)
    fs[8:16, :] = update.astype(BF16)

    for slot, (dx, dy) in enumerate(cross):
        send(fs, rf.at[slot], ft_s, ft_r, shot_at(-dy), slab_at(-dx))
    pltpu.make_async_copy(rf, rf, ft_r).wait()

    def row_inside(k):
        return jnp.where((s + k >= 0) & (s + k < shots), 1.0, 0.0).astype(F32)

    for slot, (dx, dy) in enumerate(cross):
        valid = inside(dx) * row_inside(dy)
        feat[(dy + 3) * 3 + dx + 1] = (rf[slot].astype(F32) * valid).astype(BF16)
    feat[10] = fs[...]

    def first_conv(y, carry):
        g1[...] = dot(w1[...], feat[pl.ds(3 * y, 9)].reshape(144, 128))
        row_ok = jnp.where((s + y - 2 >= 0) & (s + y - 2 < shots), 1.0, 0.0)

        def one(x, carry):
            plane = b * 8 + x - 2
            ok = jnp.where((plane >= 0) & (plane < slabs * 8), row_ok, 0.0)
            g = g1[pl.ds(pl.multiple_of(x * 192, 192), 192), :]
            value = jnp.maximum(z_combine(g, lane) + b1[...], 0.0) * ok
            h1[y, x] = value.astype(BF16)
            return carry
        lax.fori_loop(0, 12, one, 0, unroll=2)
        return carry

    lax.fori_loop(0, 5, first_conv, 0)

    def second_conv(i, carry):
        y = i // 5
        x0 = 2 * (i - 5 * y)
        halves = []
        for x in (x0, x0 + 1):
            halves.append(jnp.concatenate([h1[y + j, pl.ds(x, 3)].reshape(192, 128) for j in range(3)], axis=0))
        g = dot(wm[...], jnp.concatenate(halves, axis=1))
        row_ok = jnp.where((s + y - 1 >= 0) & (s + y - 1 < shots), 1.0, 0.0)
        for half in range(2):
            x = x0 + half
            plane = b * 8 + x - 1
            ok = jnp.where((plane >= 0) & (plane < slabs * 8), row_ok, 0.0)
            value = jnp.maximum(z_combine(g[:, 128 * half:128 * half + 128], lane) + b2[...], 0.0) * ok
            h2[y, x] = value.astype(BF16)
        return carry

    lax.fori_loop(0, 15, second_conv, 0)

    lane1 = lax.broadcasted_iota(jnp.int32, (1, 128), 1)
    for x in range(8):
        rhs = jnp.concatenate([h2[j, x:x + 3].reshape(192, 128) for j in range(3)], axis=0)
        g = dot(w3[...], rhs)
        low = jnp.where(lane1 == 0, 0.0, pltpu.roll(g[0:8], 1, 1)[0:1])
        high = jnp.where(lane1 == 127, 0.0, pltpu.roll(g[0:8], 127, 1)[2:3])
        row[x:x + 1, :] = moved[x:x + 1] + (g[1:2] + low + high + b3[0])

    for k in range(1, shots):
        send(row, ro.at[k - 1], ou_s, ou_r, shot_at(k), b)
    out[s] = row[...]
    pltpu.make_async_copy(ro, ro, ou_r).wait()
    for k in range(1, shots):
        out[shot_at(-k)] = ro[k - 1]

    for copy in sent:
        copy.wait_send()
    pltpu.make_async_copy(rt, rt, tr_s).wait()
    pltpu.make_async_copy(ri, ri, im_s).wait()
    pltpu.make_async_copy(rf, rf, ft_s).wait()
    pltpu.make_async_copy(ro, ro, ou_s).wait()


def band_weights(weight_in):
    w = weight_in.reshape(3, 3, 3, 2, 64)
    x = jnp.arange(12)[None, :]
    plane = jnp.arange(24)[None, None, :] - 8
    tap = jnp.arange(3)[:, None]
    select = (plane - (x - 2)[:, :, None] + 1 == tap[:, :, None]).astype(BF16)
    select = select.reshape(3, 12, 3, 8)
    wide = jnp.einsum("ijkco,ixdp->xkojdcp", w, select)
    return wide.reshape(12 * 192, 144)


def shards(slabs, shots, previous_field, current_field, adjoint_next, adjoint_current, velocity, wavelet, source_cell,
           receiver_cell, observed, weight_in, bias_in, weight_mid, bias_mid, weight_out, bias_out):
    w1 = band_weights(weight_in)
    wm = jnp.transpose(weight_mid.reshape(3, 3, 3, 64, 64), (2, 4, 1, 0, 3)).reshape(192, 576)
    w3 = jnp.transpose(weight_out.reshape(3, 3, 3, 64), (2, 1, 0, 3)).reshape(3, 576)
    w3 = jnp.pad(w3, ((0, 13), (0, 0)))
    vmem = pl.BlockSpec(memory_space=pltpu.VMEM)
    smem = pl.BlockSpec(memory_space=pltpu.SMEM)
    f32 = lambda *shape: pltpu.VMEM(shape, F32)
    bf = lambda *shape: pltpu.VMEM(shape, BF16)
    dma = pltpu.SemaphoreType.DMA
    scratch = [
        f32(24, 48, 128), f32(24, 48, 128), f32(24, 48, 128), f32(24, 48, 128),
        f32(48, 48, 128), f32(48, 48, 128), f32(40, 32, 128), f32(40, 32, 128), f32(40, 32, 128),
        f32(6, 8, 32, 128), f32(6, 8, 32, 128), f32(8, 32, 128), f32(32, 8, 128),
        bf(8, 32, 128), bf(4, 8, 32, 128), bf(2, 2, 8, 32, 128), bf(2, 2, 4, 32, 128),
        bf(2, 2, 8, 32, 128), bf(2, 2, 2, 8, 32, 128),
        f32(8, 256), f32(slabs - 1, 8, 256), f32(8, 256),
        bf(1536, 256), bf(256, 256), f32(256, 128), f32(32, 128), bf(256, 128), bf(128, 128),
        f32(shots - 1, 8, 128), bf(16, 128), bf(20, 16, 128), bf(21, 16, 128), f32(2304, 128),
        bf(5, 12, 64, 128), bf(3, 10, 64, 128), f32(8, 128), f32(shots - 1, 8, 128),
        dma((2, 6)), dma((2, 6)), dma((2, 2)), dma((2, 2)),
    ] + [dma] * 8
    rows, misfit = pl.pallas_call(
        functools.partial(kernel, slabs, shots),
        out_shape=(jax.ShapeDtypeStruct((shots, 8, 128), F32), jax.ShapeDtypeStruct((1, 6, 256), F32)),
        in_specs=[vmem, vmem, vmem, vmem, vmem, smem, smem, vmem, vmem, vmem, vmem, vmem, vmem, vmem, smem],
        out_specs=(vmem, vmem),
        scratch_shapes=scratch,
        compiler_params=pltpu.CompilerParams(
            collective_id=0, has_side_effects=True, vmem_limit_bytes=60 * 1024 * 1024),
    )(previous_field, current_field, adjoint_next, adjoint_current, velocity, wavelet, source_cell, receiver_cell,
      observed, w1, bias_in[:, None], wm, bias_mid[:, None], w3, bias_out)
    return jnp.swapaxes(rows, 0, 1), misfit


def solution(mesh):
    placed = (
        P("shot", "slab", None, None), P("shot", "slab", None, None), P("shot", "slab", None, None),
        P("shot", "slab", None, None), P("slab", None, None), P("shot", None), P("shot"), P("shot", None),
        P("shot", None, None), P(), P(), P(), P(), P(), P(),
    )
    return jax.shard_map(
        functools.partial(shards, mesh.shape["slab"], mesh.shape["shot"]),
        mesh=mesh,
        in_specs=placed,
        out_specs=(P("slab", None, None), P("shot", None, None)),
        check_vma=False,
    )
```

time: 693 us -> 114 us (0.16)
  the two profiles are of different devices: /device:TPU:57 before, /device:TPU:1 now
where the time goes in v1:
time: 114 us
  Pallas kernels  98.9 us (87%)
  local copies, waits for them, and re-layouts  12.1 us (11%)
  between operations  2.04 us (2%)
    pallas_call x1, Pallas kernels, shards(): pl.pallas_call(functools.partial(kernel, slabs, shots), out_shape=(jax.Sh...  98.9 us
    unnamed x15, local copies, waits for them, and re-layouts  4.12 us
    reshape x2, local copies, waits for them, and re-layouts, band_weights(): return wide.reshape(12 * 192, 144)  2.62 us

profile of v1, /device:TPU:1, one launch (start us, length us, event | category | flops | bytes accessed | tf_op | source)
XLA Modules:
  0.0 113.9 jit_solution(17498007711808709159)
XLA Ops:
  0.6 0.0 copy-start
  0.7 0.1 subtract_add_fusion
  0.7 0.6 copy-done
  1.3 0.7 convolution_bitcast_fusion
  2.1 1.4 %copy.27 = bf16[12,3,64,3,3,2,8]{2,1,0,6,5,4,3:T(4,128)(2,1)S(1)} copy(bf16[12,3,64,3,3,2,8]{2,0,5,1,3,6,4:T(8,128)(2,1)S(1)} %convolution_bitcast_fusion) | data formatting | bytes 1327104 | tf_op jit(solution)/shard_map/ijkco,ixdp->xkojdcp/transpose | solution.py:370
  3.4 0.0 copy-start.1
  3.5 1.2 %reshape.74 = bf16[2304,144]{0,1:T(8,128)(2,1)S(1)} reshape(bf16[12,3,64,3,3,2,8]{2,1,0,6,5,4,3:T(4,128)(2,1)S(1)} %copy.27) | data formatting | bytes 1327104 | tf_op jit(solution)/shard_map/reshape | solution.py:371
  4.7 0.0 copy-start.2
  4.7 0.0 copy-start.4
  4.7 0.0 copy-start.5
  4.7 0.0 copy-start.3
  4.7 1.4 %copy.31.w1 = bf16[2304,144]{1,0:T(8,128)(2,1)} copy(bf16[2304,144]{0,1:T(8,128)(2,1)S(1)} %reshape.74) | data formatting | bytes 1327104 | tf_op jit(solution)/shard_map/reshape | solution.py:371
  6.1 0.0 copy-done.1
  6.1 0.8 copy.28
  7.0 1.1 reshape.76.wm
  8.1 0.0 copy-done.2
  8.1 0.1 reshape.78
  8.2 0.6 pad.4.w3
  8.8 0.0 copy-done.4
  8.8 0.7 copy.32.b1
  9.5 0.0 copy-done.5
  9.5 0.7 copy.33.b2
  10.2 0.0 copy-done.3
  10.2 0.6 copy.30.obs
  12.1 98.9 %shard_map.158 = (f32[32,8,128]{2,1,0:T(8,128)}, f32[1,6,256]{2,1,0:T(8,128)}) custom-call(bf16[1,8,32,128]{3,2,1,0:T(8,128)(2,1)} %prev.1, bf16[1,8,32,128]{3,2,1,0:T(8,128)(2,1)} %cur.1, bf16[1,8,32,128]{3,2,1,0:T(8,128)(2,1)} %anext.1, bf16[1,8,32,128]{3,2,1,0:T(8,128)(2,1)} %acur.1, f32[8,32,128]{2,1,0:T(8,128)} %vel.1, f32[1,6]{1,0:T(1,128)} %wav.1, ...), custom_call_target="tpu_custom_call" | custom-call | tf_op jit(solution)/shard_map/pallas_call | solution.py:397
  111.0 1.6 %copy.34 = f32[8,32,128]{2,1,0:T(8,128)} copy(f32[8,32,128]{2,0,1:T(8,128)} %bitcast.25) | data formatting | bytes 262144
  112.6 1.3 %copy.35 = f32[1,6,256]{2,0,1:T(1,128)} copy(f32[1,6,256]{2,1,0:T(8,128)} %get-tuple-element.9) | data formatting | bytes 12288
  (4 shorter events, 0.0 us)
Async XLA Ops:
  0.6 0.7 copy-start
  3.4 2.7 %copy-start.1 = (bf16[27,64,64]{2,1,0:T(8,128)(2,1)S(1)}, bf16[27,64,64]{2,1,0:T(8,128)(2,1)}, u32[]{:S(2)}) copy-start(bf16[27,64,64]{2,1,0:T(8,128)(2,1)} %param.26) | copy-start | bytes 663556
  4.7 3.4 %copy-start.2 = (bf16[27,64,1]{1,0,2:T(8,128)(2,1)S(1)}, bf16[27,64,1]{1,0,2:T(8,128)(2,1)}, u32[]{:S(2)}) copy-start(bf16[27,64,1]{1,0,2:T(8,128)(2,1)} %param.28) | copy-start | bytes 10372
  4.7 4.1 %copy-start.4 = (f32[64]{0:T(128)S(1)}, f32[64]{0:T(128)}, u32[]{:S(2)}) copy-start(f32[64]{0:T(128)} %param.25) | copy-start | bytes 772
  4.7 4.8 %copy-start.5 = (f32[64]{0:T(128)S(1)}, f32[64]{0:T(128)}, u32[]{:S(2)}) copy-start(f32[64]{0:T(128)} %param.27) | copy-start | bytes 772
  4.7 5.5 %copy-start.3 = (f32[1,6,256]{2,0,1:T(1,128)S(1)}, f32[1,6,256]{2,0,1:T(1,128)}, u32[]{:S(2)}) copy-start(f32[1,6,256]{2,0,1:T(1,128)} %param.23) | copy-start | bytes 18436

commit v2 on v1

--- a/solution.py
+++ b/solution.py
@@ -42,13 +42,13 @@
 
 def kernel(
     slabs, shots,
-    prev, cur, anext, acur, vel, wav, src, rec, obs, w1, b1, wm, b2, w3, b3,
-    out, mis,
-    u0, u1, wa0, wa1, da, db, zs, js, kap, lap, hom, img, imgt,
-    sv, rv, rc, rp, sb, rb, tr, rt, mf, hot, pick, lane_hot, src_hot, bands, bandl,
-    ri, fs, rf, feat, g1, h1, h2, row, ro,
-    init_s, init_r, round_s, round_r, tr_s, tr_r, im_s, im_r, ft_s, ft_r, ou_s, ou_r,
+    wav, src, b3, *refs,
 ):
+    hbm, (out, mis), loaded, rest = refs[:12], refs[12:14], refs[14:26], refs[26:]
+    prev, cur, anext, acur, vel, rec, obs, wi, bi, wd, bd, wo = loaded
+    (
+        u0, u1, wa0, wa1, da, db, zs, js, kap, lap, hom, img, imgt, sv, vp, rv, rn, rc, rp, sb, rb, tr, rt, mf, hot, pick, lane_hot, src_hot, bands, bandl, ri, fs, rf, feat, wf, w1, wm, w3, widen, im, h1, h2, row, ro, init_s, init_r, vp_s, vp_r, rv_s, rv_r, round_s, round_r, tr_s, tr_r, im_s, im_r, ft_s, ft_r, ou_s, ou_r, load_s,
+    ) = rest
     s = lax.axis_index("shot")
     b = lax.axis_index("slab")
 
@@ -76,23 +76,34 @@
     for peer in peers:
         pl.semaphore_signal(barrier, inc=1, device_id=peer, device_id_type=MESH)
 
+    loads = [pltpu.make_async_copy(hbm[at], loaded[at], load_s.at[at]) for at in range(12)]
+    for at in (4, 1, 0, 3, 2, 5, 6, 7, 8, 9, 10, 11):
+        loads[at].start()
+    loads[4].wait()
     sv[...] = (vel[...] - MID).astype(BF16)
+    for at in (0, 1, 2, 3):
+        loads[at].wait()
     pl.semaphore_wait(barrier, len(peers))
 
+    zi = lax.rem(lax.div(s, 2), 8)
     sent = []
-    first = []
-    for side, step in ((0, 1), (1, -1)):
-        target = slab_at(step)
-        edge = pl.ds(4, 4) if step == 1 else pl.ds(0, 4)
-        for f, (now, old) in enumerate(((cur, prev), (acur, anext))):
-            first.append(send(now.at[0], rc.at[side, f], init_s.at[side, 2 * f], init_r.at[side, 2 * f], s, target))
-            first.append(send(old.at[0, edge], rp.at[side, f], init_s.at[side, 2 * f + 1], init_r.at[side, 2 * f + 1], s, target))
-        first.append(send(sv, rv.at[1 + side], init_s.at[side, 4], init_r.at[side, 4], s, target))
-    far = []
-    for side, step in ((0, 2), (1, -2)):
-        far.append(send(sv, rv.at[3 * side], init_s.at[side, 5], init_r.at[side, 5], s, slab_at(step)))
-    sent += first + far
-
+    first = ([], [])
+    for f, (now, old) in enumerate(((cur, prev), (acur, anext))):
+        for side, step in ((0, 1), (1, -1)):
+            target = slab_at(step)
+            edge = pl.ds(4, 4) if step == 1 else pl.ds(0, 4)
+            at = init_s.at[side, 2 * f], init_r.at[side, 2 * f]
+            first[f].append(send(now.at[0], rc.at[side, f], *at, s, target))
+            at = init_s.at[side, 2 * f + 1], init_r.at[side, 2 * f + 1]
+            first[f].append(send(old.at[0, edge], rp.at[side, f], *at, s, target))
+            if f == 0:
+                first[f].append(send(sv.at[edge], rn.at[side], init_s.at[side, 4], init_r.at[side, 4], s, target))
+    for slot, step in enumerate((2, 1, -1, -2)):
+        send(sv.at[zi], vp.at[slot], vp_s, vp_r, s, slab_at(step))
+    sent += first[0] + first[1]
+
+    for at in range(5, 12):
+        loads[at].wait()
     lane = lax.broadcasted_iota(jnp.int32, (64, 128), 1)
     diff = jnp.abs(lax.broadcasted_iota(jnp.int32, (128, 128), 0) - lax.broadcasted_iota(jnp.int32, (128, 128), 1))
     band = jnp.where(diff == 0, 3.0 * COEFFS[0], 0.0)
@@ -141,6 +152,51 @@
         (lax.broadcasted_iota(jnp.int32, (ROWS, 128), 0) == src_row)
         & (lax.broadcasted_iota(jnp.int32, (ROWS, 128), 1) == src_lane), 1.0, 0.0)
 
+    def iota(rows, columns, axis):
+        return lax.broadcasted_iota(jnp.int32, (rows, columns), axis)
+
+    def one_hot(condition):
+        return jnp.where(condition, 1.0, 0.0).astype(BF16)
+
+    eye64 = one_hot(iota(64, 64, 0) == iota(64, 64, 1))
+    wf[...] = jnp.zeros((96, 64), F32)
+    for t in range(27):
+        wf[2 * t:2 * t + 2, :] = wi[t].astype(F32)
+    wf[64:91, :] = wo[...].astype(F32)
+    taps_in = wf[0:64, :].astype(BF16)
+    taps_out = wf[64:96, :].astype(BF16)
+    q = iota(96, 64, 0)
+    i, j, c = (q >> 3) & 3, (q >> 1) & 3, q & 1
+    wanted = one_hot((iota(96, 64, 1) == (9 * i + 3 * j + (q >> 5)) * 2 + c) & (i < 3) & (j < 3))
+    chosen = dot(wanted, taps_in).astype(BF16)
+    w1[...] = lax.dot_general(eye64, chosen, NT, preferred_element_type=F32).astype(BF16)
+    for k in range(3):
+        for u in range(0, 9, 2):
+            pair = [wd[9 * (v % 3) + 3 * (v // 3) + k] for v in range(u, min(u + 2, 9))]
+            both = lax.dot_general(eye64, jnp.concatenate(pair, axis=0), NT, preferred_element_type=F32)
+            wm[64 * k:64 * k + 64, 64 * u:64 * (u + len(pair))] = both.astype(BF16)
+    for u in range(0, 9, 2):
+        both = jnp.zeros((16, 128), F32)
+        for v in range(u, min(u + 2, 9)):
+            wanted = one_hot((iota(16, 32, 1) == 9 * (v % 3) + 3 * (v // 3) + iota(16, 32, 0)) & (iota(16, 32, 0) < 3))
+            place = one_hot(iota(64, 128, 1) == iota(64, 128, 0) + 64 * (v - u))
+            both = both + dot(dot(wanted, taps_out).astype(BF16), place)
+        w3[:, 64 * u:min(64 * u + 128, 576)] = both[:, 0:min(128, 576 - 64 * u)].astype(BF16)
+    sub64 = iota(8, 64, 0)
+    biases = jnp.zeros((8, 64), F32)
+    for at, part in enumerate(split(bi[...], 3) + split(bd[...], 3)):
+        biases = jnp.where(sub64 == at, part.astype(F32), biases)
+    bias_col = lax.dot_general(eye64, biases.astype(BF16), NT, preferred_element_type=F32)
+    b1 = bias_col[:, 0:1] + bias_col[:, 1:2] + bias_col[:, 2:3]
+    b2 = bias_col[:, 3:4] + bias_col[:, 4:5] + bias_col[:, 5:6]
+    r, col = iota(384, 144, 0), iota(384, 144, 1)
+    group = jnp.where(col >= 48, 1, 0) + jnp.where(col >= 96, 1, 0)
+    rest = col - 48 * group
+    part_of = rest >> 4
+    widen[...] = one_hot(
+        (((r >> 1) & 3) == group) & ((r & 1) == ((rest >> 3) & 1)) & (((r >> 3) & 3) < 3)
+        & (8 * part_of + (rest & 7) == (r >> 5) + ((r >> 3) & 3) + 5))
+
     def z_pass(field, lo, n):
         for c in range(n // 8):
             x = field[lo + 8 * c:lo + 8 * c + 8, YS, :].reshape(256, 128)
@@ -165,7 +221,7 @@
     def plain(i, j, new, acc):
         return new
 
-    def forward_extra(n, keep_lo):
+    def forward_extra(n):
         weight = wav[0, n]
         first_plane = b * 8 - 8
 
@@ -184,69 +240,87 @@
 
     tr[...] = jnp.zeros((8, 256), F32)
     left, right = inside(-1), inside(1)
-    for copy in first:
-        copy.wait_recv()
-    for f, (now, old) in enumerate(((u0, wa0), (u1, wa1))):
-        now[0:8, YS, :] = rc[0, f].astype(F32) * left
-        now[16:24, YS, :] = rc[1, f].astype(F32) * right
-        old[4:8, YS, :] = rp[0, f].astype(F32) * left
-        old[16:20, YS, :] = rp[1, f].astype(F32) * right
-
-    def kappa_of(slot, valid):
-        value = (rv[slot].astype(F32) + MID) * COURANT
+
+    def kappa_of(values, valid):
+        value = (values.astype(F32) + MID) * COURANT
         return value * value * valid
 
-    kap[8:16] = kappa_of(1, left)
-    kap[24:32] = kappa_of(2, right)
-
-    for r in range(3):
+    def fill(now, from_left, from_right):
+        now[0:8, YS, :] = from_left.astype(F32) * left
+        now[16:24, YS, :] = from_right.astype(F32) * right
+
+    fields = ((u0, wa0), (u1, wa1))
+    copies = [None, None]
+
+    def round_of(r, f):
+        now, old = fields[f]
+        if r == 0:
+            for copy in first[f]:
+                copy.wait_recv()
+            fill(now, rc[0, f], rc[1, f])
+            old[4:8, YS, :] = rp[0, f].astype(F32) * left
+            old[16:20, YS, :] = rp[1, f].astype(F32) * right
+            if f == 0:
+                kap[12:16] = kappa_of(rn[0], left)
+                kap[24:28] = kappa_of(rn[1], right)
+        else:
+            for copy in copies[f]:
+                copy.wait_recv()
+            fill(now, rb[r - 1, f, 0], rb[r - 1, f, 1])
         n = 2 * r
-        z_pass(u0, 4, 16)
-        advance(u0, wa0, 4, 16, 12, forward_extra(n, 4))
-        lap[n] = zs[4:12]
-        z_pass(wa0, 8, 8)
-        advance(wa0, u0, 8, 8, 16, forward_extra(n + 1, 0))
-        lap[n + 1] = zs[0:8]
-        z_pass(u1, 4, 16)
-        advance(u1, wa1, 4, 16, 12, plain)
-        z_pass(wa1, 8, 8)
-        advance(wa1, u1, 8, 8, 16, plain)
+        z_pass(now, 4, 16)
+        advance(now, old, 4, 16, 12, plain if f else forward_extra(n))
+        if f == 0:
+            lap[n] = zs[4:12]
+        z_pass(old, 8, 8)
+        advance(old, now, 8, 8, 16, plain if f else forward_extra(n + 1))
+        if f == 0:
+            lap[n + 1] = zs[0:8]
         if r < 2:
-            sb[r, 0] = u0[8:16, YS, :].astype(BF16)
-            sb[r, 1] = u1[8:16, YS, :].astype(BF16)
-            copies = [
-                send(sb.at[r], rb.at[r, side], round_s.at[r, side], round_r.at[r, side], s, slab_at(step))
+            sb[r, f] = now[8:16, YS, :].astype(BF16)
+            copies[f] = [
+                send(sb.at[r, f], rb.at[r, f, side], round_s.at[2 * r + f, side], round_r.at[2 * r + f, side],
+                     s, slab_at(step))
                 for side, step in ((0, 1), (1, -1))]
-            sent += copies
-        sample(wa0, n)
-        sample(u0, n + 1)
-        hom[STEPS - 1 - n] = wa1[8:16, YS, :]
-        hom[STEPS - 2 - n] = u1[8:16, YS, :]
-        if r < 2:
-            for copy in copies:
-                copy.wait_recv()
-            for f, now in enumerate((u0, u1)):
-                now[0:8, YS, :] = rb[r, 0, f].astype(F32) * left
-                now[16:24, YS, :] = rb[r, 1, f].astype(F32) * right
+            sent.extend(copies[f])
+        if f == 0:
+            sample(old, n)
+            sample(now, n + 1)
+        else:
+            hom[STEPS - 1 - n] = old[8:16, YS, :]
+            hom[STEPS - 2 - n] = now[8:16, YS, :]
+
+    round_of(0, 0)
+    pltpu.make_async_copy(vp, vp, vp_r).wait()
+    for k in range(1, 8):
+        send(vp, rv.at[k - 1], rv_s, rv_r, s + 2 * (lax.rem(zi + k, 8) - zi), b)
+    round_of(0, 1)
+    round_of(1, 0)
+    round_of(1, 1)
+    round_of(2, 0)
 
     for k in range(1, slabs):
         send(tr, rt.at[k - 1], tr_s, tr_r, s, slab_at(k))
+    round_of(2, 1)
     image = hom[0] * lap[0]
     for n in range(1, STEPS):
         image = image + hom[n] * lap[n]
     img[...] = image
-    for copy in far:
-        copy.wait_recv()
-    kap[0:8] = kappa_of(0, inside(-2))
-    kap[32:40] = kappa_of(3, inside(2))
+    pltpu.make_async_copy(rv, rv, rv_r).wait()
+    near_far = ((0, inside(-2)), (8, left), (24, right), (32, inside(2)))
+    for k in range(8):
+        plane = lax.rem(zi - k + 8, 8)
+        for slot, (base, valid) in enumerate(near_far):
+            kap[base + plane] = kappa_of(rv[k - 1, slot] if k else vp[slot], valid)
     pltpu.make_async_copy(rt, rt, tr_r).wait()
     total = tr[...]
     for k in range(slabs - 1):
         total = total + rt[k]
-    traces = total[0:STEPS] - obs[0]
-    mis[0] = traces
     mf[...] = jnp.zeros((8, 256), F32)
-    mf[0:STEPS, :] = traces
+    for n in range(STEPS):
+        trace = total[n:n + 1] - obs[n]
+        mis[n] = trace
+        mf[n:n + 1, :] = trace
     amounts = jnp.zeros((256, 8), F32)
     for part in split(mf[...], 3):
         amounts = amounts + lax.dot_general(eye, part, NT, preferred_element_type=F32)
@@ -298,44 +372,50 @@
     def row_inside(k):
         return jnp.where((s + k >= 0) & (s + k < shots), 1.0, 0.0).astype(F32)
 
+    lane16 = iota(16, 128, 1)
+
+    def place_features(at, values):
+        feat[at, :, 0:128] = jnp.where(lane16 == 0, 0.0, pltpu.roll(values, 1, 1)).astype(BF16)
+        feat[at, :, 128:256] = values.astype(BF16)
+        feat[at, :, 256:384] = jnp.where(lane16 == 127, 0.0, pltpu.roll(values, 127, 1)).astype(BF16)
+
     for slot, (dx, dy) in enumerate(cross):
         valid = inside(dx) * row_inside(dy)
-        feat[(dy + 3) * 3 + dx + 1] = (rf[slot].astype(F32) * valid).astype(BF16)
-    feat[10] = fs[...]
+        place_features((dy + 3) * 3 + dx + 1, rf[slot].astype(F32) * valid)
+    place_features(10, fs[...].astype(F32))
 
     def first_conv(y, carry):
-        g1[...] = dot(w1[...], feat[pl.ds(3 * y, 9)].reshape(144, 128))
+        spread = dot(widen[...], feat[pl.ds(3 * y, 9)].reshape(144, 384)).astype(BF16)
+        for k in range(3):
+            im[:, k] = spread[:, 128 * k:128 * k + 128].reshape(12, 32, 128)
         row_ok = jnp.where((s + y - 2 >= 0) & (s + y - 2 < shots), 1.0, 0.0)
-
-        def one(x, carry):
-            plane = b * 8 + x - 2
-            ok = jnp.where((plane >= 0) & (plane < slabs * 8), row_ok, 0.0)
-            g = g1[pl.ds(pl.multiple_of(x * 192, 192), 192), :]
-            value = jnp.maximum(z_combine(g, lane) + b1[...], 0.0) * ok
-            h1[y, x] = value.astype(BF16)
-            return carry
-        lax.fori_loop(0, 12, one, 0, unroll=2)
+        for x0 in range(0, 12, 2):
+            g = dot(w1[...], jnp.concatenate([im[x0].reshape(96, 128), im[x0 + 1].reshape(96, 128)], axis=1))
+            for half in range(2):
+                plane = b * 8 + x0 + half - 2
+                ok = jnp.where((plane >= 0) & (plane < slabs * 8), row_ok, 0.0)
+                value = jnp.maximum(g[:, 128 * half:128 * half + 128] + b1, 0.0) * ok
+                h1[y, x0 + half] = value.astype(BF16)
         return carry
 
     lax.fori_loop(0, 5, first_conv, 0)
 
-    def second_conv(i, carry):
-        y = i // 5
-        x0 = 2 * (i - 5 * y)
-        halves = []
-        for x in (x0, x0 + 1):
-            halves.append(jnp.concatenate([h1[y + j, pl.ds(x, 3)].reshape(192, 128) for j in range(3)], axis=0))
-        g = dot(wm[...], jnp.concatenate(halves, axis=1))
+    def second_conv(y, carry):
         row_ok = jnp.where((s + y - 1 >= 0) & (s + y - 1 < shots), 1.0, 0.0)
-        for half in range(2):
-            x = x0 + half
-            plane = b * 8 + x - 1
-            ok = jnp.where((plane >= 0) & (plane < slabs * 8), row_ok, 0.0)
-            value = jnp.maximum(z_combine(g[:, 128 * half:128 * half + 128], lane) + b2[...], 0.0) * ok
-            h2[y, x] = value.astype(BF16)
+        for x0 in range(0, 10, 2):
+            halves = []
+            for x in (x0, x0 + 1):
+                halves.append(jnp.concatenate([h1[y + j, x:x + 3].reshape(192, 128) for j in range(3)], axis=0))
+            g = dot(wm[...], jnp.concatenate(halves, axis=1))
+            for half in range(2):
+                x = x0 + half
+                plane = b * 8 + x - 1
+                ok = jnp.where((plane >= 0) & (plane < slabs * 8), row_ok, 0.0)
+                value = jnp.maximum(z_combine(g[:, 128 * half:128 * half + 128], lane) + b2, 0.0) * ok
+                h2[y, x] = value.astype(BF16)
         return carry
 
-    lax.fori_loop(0, 15, second_conv, 0)
+    lax.fori_loop(0, 3, second_conv, 0)
 
     lane1 = lax.broadcasted_iota(jnp.int32, (1, 128), 1)
     for x in range(8):
@@ -354,57 +434,46 @@
 
     for copy in sent:
         copy.wait_send()
+    pltpu.make_async_copy(vp, vp, vp_s).wait()
+    pltpu.make_async_copy(rv, rv, rv_s).wait()
     pltpu.make_async_copy(rt, rt, tr_s).wait()
     pltpu.make_async_copy(ri, ri, im_s).wait()
     pltpu.make_async_copy(rf, rf, ft_s).wait()
     pltpu.make_async_copy(ro, ro, ou_s).wait()
 
 
-def band_weights(weight_in):
-    w = weight_in.reshape(3, 3, 3, 2, 64)
-    x = jnp.arange(12)[None, :]
-    plane = jnp.arange(24)[None, None, :] - 8
-    tap = jnp.arange(3)[:, None]
-    select = (plane - (x - 2)[:, :, None] + 1 == tap[:, :, None]).astype(BF16)
-    select = select.reshape(3, 12, 3, 8)
-    wide = jnp.einsum("ijkco,ixdp->xkojdcp", w, select)
-    return wide.reshape(12 * 192, 144)
-
-
 def shards(slabs, shots, previous_field, current_field, adjoint_next, adjoint_current, velocity, wavelet, source_cell,
            receiver_cell, observed, weight_in, bias_in, weight_mid, bias_mid, weight_out, bias_out):
-    w1 = band_weights(weight_in)
-    wm = jnp.transpose(weight_mid.reshape(3, 3, 3, 64, 64), (2, 4, 1, 0, 3)).reshape(192, 576)
-    w3 = jnp.transpose(weight_out.reshape(3, 3, 3, 64), (2, 1, 0, 3)).reshape(3, 576)
-    w3 = jnp.pad(w3, ((0, 13), (0, 0)))
     vmem = pl.BlockSpec(memory_space=pltpu.VMEM)
     smem = pl.BlockSpec(memory_space=pltpu.SMEM)
     f32 = lambda *shape: pltpu.VMEM(shape, F32)
     bf = lambda *shape: pltpu.VMEM(shape, BF16)
     dma = pltpu.SemaphoreType.DMA
-    scratch = [
+    arrays = (previous_field, current_field, adjoint_next, adjoint_current, velocity, receiver_cell,
+              jnp.swapaxes(observed, 0, 1), weight_in, bias_in[None], weight_mid, bias_mid[None], weight_out.reshape(27, 64))
+    scratch = [pltpu.VMEM(a.shape, a.dtype) for a in arrays] + [
         f32(24, 48, 128), f32(24, 48, 128), f32(24, 48, 128), f32(24, 48, 128),
         f32(48, 48, 128), f32(48, 48, 128), f32(40, 32, 128), f32(40, 32, 128), f32(40, 32, 128),
         f32(6, 8, 32, 128), f32(6, 8, 32, 128), f32(8, 32, 128), f32(32, 8, 128),
-        bf(8, 32, 128), bf(4, 8, 32, 128), bf(2, 2, 8, 32, 128), bf(2, 2, 4, 32, 128),
+        bf(8, 32, 128), bf(4, 32, 128), bf(7, 4, 32, 128), bf(2, 4, 32, 128), bf(2, 2, 8, 32, 128), bf(2, 2, 4, 32, 128),
         bf(2, 2, 8, 32, 128), bf(2, 2, 2, 8, 32, 128),
         f32(8, 256), f32(slabs - 1, 8, 256), f32(8, 256),
         bf(1536, 256), bf(256, 256), f32(256, 128), f32(32, 128), bf(256, 128), bf(128, 128),
-        f32(shots - 1, 8, 128), bf(16, 128), bf(20, 16, 128), bf(21, 16, 128), f32(2304, 128),
+        f32(shots - 1, 8, 128), bf(16, 128), bf(20, 16, 128), bf(21, 16, 384),
+        f32(96, 64), bf(64, 96), bf(192, 576), bf(16, 576), bf(384, 144), bf(12, 3, 32, 128),
         bf(5, 12, 64, 128), bf(3, 10, 64, 128), f32(8, 128), f32(shots - 1, 8, 128),
-        dma((2, 6)), dma((2, 6)), dma((2, 2)), dma((2, 2)),
-    ] + [dma] * 8
+        dma((2, 5)), dma((2, 5)), dma, dma, dma, dma, dma((4, 2)), dma((4, 2)),
+    ] + [dma] * 8 + [dma((12,))]
     rows, misfit = pl.pallas_call(
         functools.partial(kernel, slabs, shots),
-        out_shape=(jax.ShapeDtypeStruct((shots, 8, 128), F32), jax.ShapeDtypeStruct((1, 6, 256), F32)),
-        in_specs=[vmem, vmem, vmem, vmem, vmem, smem, smem, vmem, vmem, vmem, vmem, vmem, vmem, vmem, smem],
+        out_shape=(jax.ShapeDtypeStruct((shots, 8, 128), F32), jax.ShapeDtypeStruct((STEPS, 1, 256), F32)),
+        in_specs=[smem, smem, smem] + [pl.BlockSpec(memory_space=pl.ANY)] * 12,
         out_specs=(vmem, vmem),
         scratch_shapes=scratch,
         compiler_params=pltpu.CompilerParams(
             collective_id=0, has_side_effects=True, vmem_limit_bytes=60 * 1024 * 1024),
-    )(previous_field, current_field, adjoint_next, adjoint_current, velocity, wavelet, source_cell, receiver_cell,
-      observed, w1, bias_in[:, None], wm, bias_mid[:, None], w3, bias_out)
-    return jnp.swapaxes(rows, 0, 1), misfit
+    )(wavelet, source_cell, bias_out, *arrays)
+    return jnp.swapaxes(rows, 0, 1), jnp.swapaxes(misfit, 0, 1)
 
 
 def solution(mesh):

time: 114 us -> 85.4 us (0.75)
  Pallas kernels: 98.9 us -> 81.1 us
  local copies, waits for them, and re-layouts: 12.1 us -> 2.19 us
    pallas_call x1, Pallas kernels: 98.9 us -> 81.1 us  [shards(): pl.pallas_call(functools.partial(kernel, slabs, shots), out_shape=(jax.Sh...]
    reshape x7 -> x0, local copies, waits for them, and re-layouts: 4.65 us -> none  [the longest x2 2.62 us: band_weights(): return wide.reshape(12 * 192, 144)]
    unnamed x15 -> x4, local copies, waits for them, and re-layouts: 4.12 us -> 2.19 us
    broadcast_in_dim x2 -> x0, local copies, waits for them, and re-layouts: 1.41 us -> none  [the longest x1 0.71 us: shards(): bias_in[:, None]]
    transpose x1 -> x0, local copies, waits for them, and re-layouts: 1.37 us -> none  [band_weights(): wide = jnp.einsum('ijkco,ixdp->xkojdcp', w, select)]
where the time goes in v2:
time: 85.4 us; the launch traced here: 85.2 us
  Pallas kernels  81.1 us (95%)
  local copies, waits for them, and re-layouts  2.19 us (3%)
  between operations  1.94 us (2%)
    pallas_call x1, Pallas kernels, shards(): pl.pallas_call(functools.partial(kernel, slabs, shots), out_shape=(jax.Sh...  81.1 us
    unnamed x4, local copies, waits for them, and re-layouts  2.19 us

profile of v2, /device:TPU:1, one launch (start us, length us, event | category | flops | bytes accessed | tf_op | source)
XLA Modules:
  0.0 85.2 jit_solution(2402056015535907954)
XLA Ops:
  1.9 81.1 %shard_map.158 = (f32[32,8,128]{2,1,0:T(8,128)}, f32[6,1,256]{2,1,0:T(1,128)}) custom-call(f32[1,6]{1,0:T(1,128)} %wav.1, s32[1]{0:T(128)S(6)} %copy.19.src, f32[1]{0:T(128)S(6)} %copy.20.b3, bf16[1,8,32,128]{3,2,1,0:T(8,128)(2,1)} %refs_0_.1, bf16[1,8,32,128]{3,2,1,0:T(8,128)(2,1)} %refs_1_.1, bf16[1,8,32,128]{3,2,1,0:T(8,128)(2,1)} %refs_2_.1, ...), custom_call_target="tpu_custom_call" | custom-call | tf_op jit(solution)/shard_map/pallas_call | solution.py:467
  83.0 0.0 copy-start
  83.0 1.6 %copy.17 = f32[8,32,128]{2,1,0:T(8,128)} copy(f32[8,32,128]{2,0,1:T(8,128)} %bitcast.6) | data formatting | bytes 262144
  84.6 0.0 copy-done
  84.6 0.6 copy.21
Async XLA Ops:
  83.0 1.6 %copy-start = (f32[6,1,256]{2,1,0:T(1,128)S(1)}, f32[6,1,256]{2,1,0:T(1,128)}, u32[]{:S(2)}) copy-start(f32[6,1,256]{2,1,0:T(1,128)} %get-tuple-element.5) | copy-start | bytes 18436

commit v3 on v2

--- a/solution.py
+++ b/solution.py
@@ -47,7 +47,8 @@
     hbm, (out, mis), loaded, rest = refs[:12], refs[12:14], refs[14:26], refs[26:]
     prev, cur, anext, acur, vel, rec, obs, wi, bi, wd, bd, wo = loaded
     (
-        u0, u1, wa0, wa1, da, db, zs, js, kap, lap, hom, img, imgt, sv, vp, rv, rn, rc, rp, sb, rb, tr, rt, mf, hot, pick, lane_hot, src_hot, bands, bandl, ri, fs, rf, feat, wf, w1, wm, w3, widen, im, h1, h2, row, ro, init_s, init_r, vp_s, vp_r, rv_s, rv_r, round_s, round_r, tr_s, tr_r, im_s, im_r, ft_s, ft_r, ou_s, ou_r, load_s,
+        u0, u1, wa0, wa1, da, db, zs, js, kap, lap, hom, img, imgt, ip, chip_sum, sv, vp, rv, rn, rc, rp, sb, rb, tr, rt, mf, hot, pick, lane_hot, src_hot, bands, bandl, ri, fs, rf, feat, wf, w1, wm, w3, widen, im, h1, h2, row, ro, init_s, init_r, vp_s, vp_r, rv_s, rv_r, round_s, round_r, tr_s, tr_r, im_s, im_r, ft_s, ft_r, ou_s, ou_r, load_s, ip_s, ip_r,
+        token_slab2, token_slab4, token_z, token_core, token_half, token_beside,
     ) = rest
     s = lax.axis_index("shot")
     b = lax.axis_index("slab")
@@ -68,11 +69,24 @@
         copy.start()
         return copy
 
+    cross = [(dx, dr) for dr in range(-2, 3) for dx in (-1, 0, 1) if (dx, dr) != (0, 0)]
+
     barrier = pltpu.get_barrier_semaphore()
-    peers = [(s, slab_at(k)) for k in range(1, slabs)]
-    peers += [(shot_at(k), b) for k in range(1, shots)]
-    cross = [(dx, dy) for dy in range(-3, 4) for dx in (-1, 0, 1) if (dx, dy) != (0, 0)]
-    peers += [(shot_at(dy), slab_at(dx)) for dx, dy in cross if dx != 0 and dy != 0]
+    zi = lax.rem(lax.div(s, 2), 8)
+    pair = lax.rem(s, 16)
+    half = s - pair
+
+    def z_at(k):
+        return s + 2 * (lax.rem(zi + k + 8, 8) - zi)
+
+    core_twin = s + 1 - 2 * lax.rem(s, 2)
+    peers = [(s, slab_at(k)) for k in (-2, -1, 1, 2)] + [(z_at(k), b) for k in (-2, -1, 1, 2)]
+    peers += [(core_twin, b), (shot_at(16), b)]
+
+    def tell(token, others):
+        for other in others:
+            pl.semaphore_signal(token, inc=1, device_id=other, device_id_type=MESH)
+
     for peer in peers:
         pl.semaphore_signal(barrier, inc=1, device_id=peer, device_id_type=MESH)
 
@@ -84,11 +98,14 @@
     for at in (0, 1, 2, 3):
         loads[at].wait()
     pl.semaphore_wait(barrier, len(peers))
-
-    zi = lax.rem(lax.div(s, 2), 8)
+    tell(token_slab2, [(s, slab_at(-2)), (s, slab_at(2))])
+    tell(token_z, [(z_at(-2), b), (z_at(2), b)])
+
     sent = []
     first = ([], [])
-    for f, (now, old) in enumerate(((cur, prev), (acur, anext))):
+
+    def send_first(f):
+        now, old = ((cur, prev), (acur, anext))[f]
         for side, step in ((0, 1), (1, -1)):
             target = slab_at(step)
             edge = pl.ds(4, 4) if step == 1 else pl.ds(0, 4)
@@ -98,9 +115,8 @@
             first[f].append(send(old.at[0, edge], rp.at[side, f], *at, s, target))
             if f == 0:
                 first[f].append(send(sv.at[edge], rn.at[side], init_s.at[side, 4], init_r.at[side, 4], s, target))
-    for slot, step in enumerate((2, 1, -1, -2)):
-        send(sv.at[zi], vp.at[slot], vp_s, vp_r, s, slab_at(step))
-    sent += first[0] + first[1]
+
+    send_first(0)
 
     for at in range(5, 12):
         loads[at].wait()
@@ -172,9 +188,9 @@
     w1[...] = lax.dot_general(eye64, chosen, NT, preferred_element_type=F32).astype(BF16)
     for k in range(3):
         for u in range(0, 9, 2):
-            pair = [wd[9 * (v % 3) + 3 * (v // 3) + k] for v in range(u, min(u + 2, 9))]
-            both = lax.dot_general(eye64, jnp.concatenate(pair, axis=0), NT, preferred_element_type=F32)
-            wm[64 * k:64 * k + 64, 64 * u:64 * (u + len(pair))] = both.astype(BF16)
+            blocks = [wd[9 * (v % 3) + 3 * (v // 3) + k] for v in range(u, min(u + 2, 9))]
+            both = lax.dot_general(eye64, jnp.concatenate(blocks, axis=0), NT, preferred_element_type=F32)
+            wm[64 * k:64 * k + 64, 64 * u:64 * (u + len(blocks))] = both.astype(BF16)
     for u in range(0, 9, 2):
         both = jnp.zeros((16, 128), F32)
         for v in range(u, min(u + 2, 9)):
@@ -197,6 +213,11 @@
         (((r >> 1) & 3) == group) & ((r & 1) == ((rest >> 3) & 1)) & (((r >> 3) & 3) < 3)
         & (8 * part_of + (rest & 7) == (r >> 5) + ((r >> 3) & 3) + 5))
 
+    send_first(1)
+    for slot, step in enumerate((2, 1, -1, -2)):
+        send(sv.at[zi], vp.at[slot], vp_s, vp_r, s, slab_at(step))
+    sent += first[0] + first[1]
+
     def z_pass(field, lo, n):
         for c in range(n // 8):
             x = field[lo + 8 * c:lo + 8 * c + 8, YS, :].reshape(256, 128)
@@ -205,30 +226,36 @@
             zs[8 * c:8 * c + 8] = z.reshape(8, ROWS, 128)
 
     def advance(field, old, lo, n, kap_lo, extra):
-        def one(i, carry):
-            j = lo + i
-            here = field[j, YS, :]
-            acc = zs[i]
-            for m in range(1, 5):
-                around = (field[j + m, YS, :] + field[j - m, YS, :]) + (
-                    field[j, TOP + m:TOP + m + ROWS, :] + field[j, TOP - m:TOP - m + ROWS, :])
-                acc = acc + COEFFS[m] * around
-            new = 2.0 * here - old[j, YS, :] + kap[kap_lo + i] * acc
-            old[j, YS, :] = extra(i, j, new, acc)
+        def four(g, carry):
+            i0 = 4 * g
+            j0 = lo + i0
+            for q in range(ROWS // 8):
+                rows = slice(8 * q, 8 * q + 8)
+                window = [field[j0 + k - 4, TOP + 8 * q:TOP + 8 * q + 8, :] for k in range(12)]
+                for p in range(4):
+                    acc = zs[i0 + p, rows, :]
+                    for m in range(1, 5):
+                        at = TOP + 8 * q
+                        around = (window[p + 4 + m] + window[p + 4 - m]) + (
+                            field[j0 + p, at + m:at + m + 8, :] + field[j0 + p, at - m:at - m + 8, :])
+                        acc = acc + COEFFS[m] * around
+                    ys = slice(TOP + 8 * q, TOP + 8 * q + 8)
+                    new = 2.0 * window[p + 4] - old[j0 + p, ys, :] + kap[kap_lo + i0 + p, rows, :] * acc
+                    old[j0 + p, ys, :] = extra(i0 + p, j0 + p, rows, new, acc)
             return carry
-        lax.fori_loop(0, n, one, 0, unroll=2)
-
-    def plain(i, j, new, acc):
+        lax.fori_loop(0, n // 4, four, 0)
+
+    def plain(i, j, rows, new, acc):
         return new
 
     def forward_extra(n):
         weight = wav[0, n]
         first_plane = b * 8 - 8
 
-        def extra(i, j, new, acc):
-            zs[i] = acc
+        def extra(i, j, rows, new, acc):
+            zs[i, rows, :] = acc
             amount = jnp.where(src_plane == first_plane + j, weight, 0.0)
-            return new + src_hot[...] * amount
+            return new + src_hot[rows, :] * amount
         return extra
 
     def sample(field, n):
@@ -291,13 +318,22 @@
             hom[STEPS - 2 - n] = now[8:16, YS, :]
 
     round_of(0, 0)
+    pl.semaphore_wait(token_slab2, 2)
+    tell(token_slab4, [(s, slab_at(-4)), (s, slab_at(4))])
+    pl.semaphore_wait(token_z, 2)
+    tell(token_core, [(core_twin, b)])
     pltpu.make_async_copy(vp, vp, vp_r).wait()
     for k in range(1, 8):
-        send(vp, rv.at[k - 1], rv_s, rv_r, s + 2 * (lax.rem(zi + k, 8) - zi), b)
+        send(vp, rv.at[k - 1], rv_s, rv_r, z_at(k), b)
     round_of(0, 1)
     round_of(1, 0)
+    pl.semaphore_wait(token_slab4, 2)
+    pl.semaphore_wait(token_core, 1)
+    tell(token_half, [(shot_at(16), b)])
     round_of(1, 1)
     round_of(2, 0)
+    pl.semaphore_wait(token_half, 1)
+    tell(token_beside, [(s, slab_at(-1)), (s, slab_at(1))])
 
     for k in range(1, slabs):
         send(tr, rt.at[k - 1], tr_s, tr_r, s, slab_at(k))
@@ -337,8 +373,8 @@
         da[8 * c:8 * c + 8, YS, :] = values
     img[...] += da[20:28, YS, :] * lap[5]
 
-    def with_misfit(i, j, new, acc):
-        return new + js[i]
+    def with_misfit(i, j, rows, new, acc):
+        return new + js[i, rows, :]
 
     near, old = da, db
     for n in range(4, -1, -1):
@@ -351,27 +387,37 @@
         near, old = old, near
         img[...] += near[20:28, YS, :] * lap[n]
 
-    imgt[...] = jnp.swapaxes(img[...], 0, 1)
-    for k in range(1, shots):
-        send(imgt.at[shot_at(k)], ri.at[k - 1], im_s, im_r, shot_at(k), b)
-    mine = lax.broadcasted_iota(jnp.int32, (8, ROWS, 128), 1) == s
-    own_velocity = jnp.sum(jnp.where(mine, vel[...], 0.0), axis=1)
-    pltpu.make_async_copy(ri, ri, im_r).wait()
-    summed = imgt[s]
-    for k in range(shots - 1):
+    by_row = jnp.swapaxes(img[...], 0, 1).reshape(8, 2, 16, 128)
+    for core in range(2):
+        imgt[core] = by_row[:, core]
+    core = lax.rem(s, 2)
+    chip = lax.div(s, 2)
+    chips = shots // 2
+    swap = send(imgt.at[1 - core], ip, ip_s, ip_r, core_twin, b)
+    sent.append(swap)
+    swap.wait_recv()
+    chip_sum[...] = imgt[core] + ip[...]
+    for k in range(1, chips):
+        target = lax.rem(chip + k, chips)
+        send(chip_sum.at[lax.rem(target, 8)], ri.at[chip], im_s, im_r, 2 * target + core, b)
+    ri[chip] = chip_sum[zi]
+    row_of = lax.broadcasted_iota(jnp.int32, (8, ROWS, 128), 1)
+    own_velocity = jnp.concatenate(
+        [jnp.sum(jnp.where(row_of == 2 * pair + y, vel[...], 0.0), axis=1) for y in range(2)], axis=0)
+    pl.semaphore_wait(token_beside, 2)
+    pltpu.make_async_copy(ri.at[0:chips - 1], ri.at[0:chips - 1], im_r).wait()
+    summed = ri[0]
+    for k in range(1, chips):
         summed = summed + ri[k]
     update = RATE * (summed / shots)
     moved = own_velocity - update
-    fs[0:8, :] = (moved - CENTER).astype(BF16)
-    fs[8:16, :] = update.astype(BF16)
-
-    for slot, (dx, dy) in enumerate(cross):
-        send(fs, rf.at[slot], ft_s, ft_r, shot_at(-dy), slab_at(-dx))
+    centered = moved - CENTER
+    for y in range(2):
+        fs[y] = jnp.concatenate([centered[8 * y:8 * y + 8], update[8 * y:8 * y + 8]], axis=0).astype(BF16)
+
+    for slot, (dx, dr) in enumerate(cross):
+        send(fs, rf.at[slot], ft_s, ft_r, half + lax.rem(pair - dr + 16, 16), slab_at(-dx))
     pltpu.make_async_copy(rf, rf, ft_r).wait()
-
-    def row_inside(k):
-        return jnp.where((s + k >= 0) & (s + k < shots), 1.0, 0.0).astype(F32)
-
     lane16 = iota(16, 128, 1)
 
     def place_features(at, values):
@@ -379,16 +425,21 @@
         feat[at, :, 128:256] = values.astype(BF16)
         feat[at, :, 256:384] = jnp.where(lane16 == 127, 0.0, pltpu.roll(values, 127, 1)).astype(BF16)
 
-    for slot, (dx, dy) in enumerate(cross):
-        valid = inside(dx) * row_inside(dy)
-        place_features((dy + 3) * 3 + dx + 1, rf[slot].astype(F32) * valid)
-    place_features(10, fs[...].astype(F32))
+    def row_inside(k):
+        return jnp.where((2 * pair + k >= 0) & (2 * pair + k < ROWS), 1.0, 0.0).astype(F32)
+
+    for slot, (dx, dr) in enumerate(cross):
+        valid = inside(dx) * row_inside(2 * dr)
+        for y in range(2):
+            place_features((2 * dr + 4 + y) * 3 + dx + 1, rf[slot, y].astype(F32) * valid)
+    for y in range(2):
+        place_features((4 + y) * 3 + 1, fs[y].astype(F32))
 
     def first_conv(y, carry):
-        spread = dot(widen[...], feat[pl.ds(3 * y, 9)].reshape(144, 384)).astype(BF16)
+        spread = dot(widen[...], feat[pl.ds(3 * y + 3, 9)].reshape(144, 384)).astype(BF16)
         for k in range(3):
             im[:, k] = spread[:, 128 * k:128 * k + 128].reshape(12, 32, 128)
-        row_ok = jnp.where((s + y - 2 >= 0) & (s + y - 2 < shots), 1.0, 0.0)
+        row_ok = row_inside(y - 2)
         for x0 in range(0, 12, 2):
             g = dot(w1[...], jnp.concatenate([im[x0].reshape(96, 128), im[x0 + 1].reshape(96, 128)], axis=1))
             for half in range(2):
@@ -398,10 +449,10 @@
                 h1[y, x0 + half] = value.astype(BF16)
         return carry
 
-    lax.fori_loop(0, 5, first_conv, 0)
+    lax.fori_loop(0, 6, first_conv, 0)
 
     def second_conv(y, carry):
-        row_ok = jnp.where((s + y - 1 >= 0) & (s + y - 1 < shots), 1.0, 0.0)
+        row_ok = row_inside(y - 1)
         for x0 in range(0, 10, 2):
             halves = []
             for x in (x0, x0 + 1):
@@ -415,29 +466,35 @@
                 h2[y, x] = value.astype(BF16)
         return carry
 
-    lax.fori_loop(0, 3, second_conv, 0)
+    lax.fori_loop(0, 4, second_conv, 0)
 
     lane1 = lax.broadcasted_iota(jnp.int32, (1, 128), 1)
-    for x in range(8):
-        rhs = jnp.concatenate([h2[j, x:x + 3].reshape(192, 128) for j in range(3)], axis=0)
-        g = dot(w3[...], rhs)
-        low = jnp.where(lane1 == 0, 0.0, pltpu.roll(g[0:8], 1, 1)[0:1])
-        high = jnp.where(lane1 == 127, 0.0, pltpu.roll(g[0:8], 127, 1)[2:3])
-        row[x:x + 1, :] = moved[x:x + 1] + (g[1:2] + low + high + b3[0])
-
-    for k in range(1, shots):
-        send(row, ro.at[k - 1], ou_s, ou_r, shot_at(k), b)
-    out[s] = row[...]
+    for y in range(2):
+        for x in range(0, 8, 2):
+            halves = []
+            for at in (x, x + 1):
+                halves.append(jnp.concatenate([h2[y + j, at:at + 3].reshape(192, 128) for j in range(3)], axis=0))
+            pair_g = dot(w3[...], jnp.concatenate(halves, axis=1))
+            for at in range(2):
+                g = pair_g[0:8, 128 * at:128 * at + 128]
+                low = jnp.where(lane1 == 0, 0.0, pltpu.roll(g, 1, 1)[0:1])
+                high = jnp.where(lane1 == 127, 0.0, pltpu.roll(g, 127, 1)[2:3])
+                i = 8 * y + x + at
+                row[i:i + 1, :] = moved[i:i + 1] + (g[1:2] + low + high + b3[0])
+
+    for k in range(1, 16):
+        send(row, ro.at[k - 1], ou_s, ou_r, half + lax.rem(pair + k, 16), b)
+    out[pair] = row[...]
     pltpu.make_async_copy(ro, ro, ou_r).wait()
-    for k in range(1, shots):
-        out[shot_at(-k)] = ro[k - 1]
+    for k in range(1, 16):
+        out[lax.rem(pair - k + 16, 16)] = ro[k - 1]
 
     for copy in sent:
         copy.wait_send()
     pltpu.make_async_copy(vp, vp, vp_s).wait()
     pltpu.make_async_copy(rv, rv, rv_s).wait()
     pltpu.make_async_copy(rt, rt, tr_s).wait()
-    pltpu.make_async_copy(ri, ri, im_s).wait()
+    pltpu.make_async_copy(ri.at[0:chips - 1], ri.at[0:chips - 1], im_s).wait()
     pltpu.make_async_copy(rf, rf, ft_s).wait()
     pltpu.make_async_copy(ro, ro, ou_s).wait()
 
@@ -454,26 +511,26 @@
     scratch = [pltpu.VMEM(a.shape, a.dtype) for a in arrays] + [
         f32(24, 48, 128), f32(24, 48, 128), f32(24, 48, 128), f32(24, 48, 128),
         f32(48, 48, 128), f32(48, 48, 128), f32(40, 32, 128), f32(40, 32, 128), f32(40, 32, 128),
-        f32(6, 8, 32, 128), f32(6, 8, 32, 128), f32(8, 32, 128), f32(32, 8, 128),
+        f32(6, 8, 32, 128), f32(6, 8, 32, 128), f32(8, 32, 128), f32(2, 8, 16, 128), f32(8, 16, 128), f32(8, 16, 128),
         bf(8, 32, 128), bf(4, 32, 128), bf(7, 4, 32, 128), bf(2, 4, 32, 128), bf(2, 2, 8, 32, 128), bf(2, 2, 4, 32, 128),
         bf(2, 2, 8, 32, 128), bf(2, 2, 2, 8, 32, 128),
         f32(8, 256), f32(slabs - 1, 8, 256), f32(8, 256),
         bf(1536, 256), bf(256, 256), f32(256, 128), f32(32, 128), bf(256, 128), bf(128, 128),
-        f32(shots - 1, 8, 128), bf(16, 128), bf(20, 16, 128), bf(21, 16, 384),
+        f32(shots // 2, 16, 128), bf(2, 16, 128), bf(14, 2, 16, 128), bf(30, 16, 384),
         f32(96, 64), bf(64, 96), bf(192, 576), bf(16, 576), bf(384, 144), bf(12, 3, 32, 128),
-        bf(5, 12, 64, 128), bf(3, 10, 64, 128), f32(8, 128), f32(shots - 1, 8, 128),
+        bf(6, 12, 64, 128), bf(4, 10, 64, 128), f32(16, 128), f32(15, 16, 128),
         dma((2, 5)), dma((2, 5)), dma, dma, dma, dma, dma((4, 2)), dma((4, 2)),
-    ] + [dma] * 8 + [dma((12,))]
+    ] + [dma] * 8 + [dma((12,)), dma, dma] + [pltpu.SemaphoreType.REGULAR] * 6
     rows, misfit = pl.pallas_call(
         functools.partial(kernel, slabs, shots),
-        out_shape=(jax.ShapeDtypeStruct((shots, 8, 128), F32), jax.ShapeDtypeStruct((STEPS, 1, 256), F32)),
+        out_shape=(jax.ShapeDtypeStruct((16, 16, 128), F32), jax.ShapeDtypeStruct((STEPS, 1, 256), F32)),
         in_specs=[smem, smem, smem] + [pl.BlockSpec(memory_space=pl.ANY)] * 12,
         out_specs=(vmem, vmem),
         scratch_shapes=scratch,
         compiler_params=pltpu.CompilerParams(
             collective_id=0, has_side_effects=True, vmem_limit_bytes=60 * 1024 * 1024),
     )(wavelet, source_cell, bias_out, *arrays)
-    return jnp.swapaxes(rows, 0, 1), jnp.swapaxes(misfit, 0, 1)
+    return jnp.swapaxes(rows.reshape(ROWS, 8, 128), 0, 1), jnp.swapaxes(misfit, 0, 1)
 
 
 def solution(mesh):

time: 85.4 us -> 83.7 us (0.980)
  Pallas kernels: 81.1 us -> 79.4 us
    pallas_call x1, Pallas kernels: 81.1 us -> 79.4 us  [shards(): pl.pallas_call(functools.partial(kernel, slabs, shots), out_shape=(jax.Sh...]
    reshape x0 -> x1, local copies, waits for them, and re-layouts: none -> 1.59 us  [shards(): rows.reshape(ROWS, 8, 128)]
    unnamed x4 -> x3, local copies, waits for them, and re-layouts: 2.19 us -> 0.6 us
where the time goes in v3:
time: 83.7 us; the launch traced here: 83.5 us
  Pallas kernels  79.4 us (95%)
  local copies, waits for them, and re-layouts  2.19 us (3%)
  between operations  1.94 us (2%)
    pallas_call x1, Pallas kernels, shards(): pl.pallas_call(functools.partial(kernel, slabs, shots), out_shape=(jax.Sh...  79.4 us

profile of v3, /device:TPU:1, one launch (start us, length us, event | category | flops | bytes accessed | tf_op | source)
XLA Modules:
  0.0 83.5 jit_solution(16809983753457760854)
XLA Ops:
  1.9 79.4 %shard_map.158 = (f32[16,16,128]{2,1,0:T(8,128)}, f32[6,1,256]{2,1,0:T(1,128)}) custom-call(f32[1,6]{1,0:T(1,128)} %wav.1, s32[1]{0:T(128)S(6)} %copy.21.src, f32[1]{0:T(128)S(6)} %copy.22.b3, bf16[1,8,32,128]{3,2,1,0:T(8,128)(2,1)} %refs_0_.1, bf16[1,8,32,128]{3,2,1,0:T(8,128)(2,1)} %refs_1_.1, bf16[1,8,32,128]{3,2,1,0:T(8,128)(2,1)} %refs_2_.1, ...), custom_call_target="tpu_custom_call" | custom-call | tf_op jit(solution)/shard_map/pallas_call | solution.py:524
  81.3 0.0 copy-start
  81.3 1.6 %copy.19 = f32[32,8,128]{2,0,1:T(8,128)} copy(f32[32,8,128]{2,1,0:T(8,128)} %bitcast.10) | data formatting | bytes 262144 | tf_op jit(solution)/shard_map/reshape | solution.py:533
  82.9 0.0 copy-done
  82.9 0.6 copy.23
Async XLA Ops:
  81.3 1.6 %copy-start = (f32[6,1,256]{2,1,0:T(1,128)S(1)}, f32[6,1,256]{2,1,0:T(1,128)}, u32[]{:S(2)}) copy-start(f32[6,1,256]{2,1,0:T(1,128)} %get-tuple-element.5) | copy-start | bytes 18436

commit v4 on v3

--- a/solution.py
+++ b/solution.py
@@ -47,7 +47,7 @@
     hbm, (out, mis), loaded, rest = refs[:12], refs[12:14], refs[14:26], refs[26:]
     prev, cur, anext, acur, vel, rec, obs, wi, bi, wd, bd, wo = loaded
     (
-        u0, u1, wa0, wa1, da, db, zs, js, kap, lap, hom, img, imgt, ip, chip_sum, sv, vp, rv, rn, rc, rp, sb, rb, tr, rt, mf, hot, pick, lane_hot, src_hot, bands, bandl, ri, fs, rf, feat, wf, w1, wm, w3, widen, im, h1, h2, row, ro, init_s, init_r, vp_s, vp_r, rv_s, rv_r, round_s, round_r, tr_s, tr_r, im_s, im_r, ft_s, ft_r, ou_s, ou_r, load_s, ip_s, ip_r,
+        u0, u1, wa0, wa1, da, db, zs, js, kap, lap, hom, img, imgt, ip, chip_sum, sv, vp, rv, rn, rc, rp, sb, rb, tr, rt, rl, mf, hot, pick, lane_hot, src_hot, bands, bandl, ri, fs, fe, rf, re, feat, wf, w1, wm, w3, band1, h1, h2, row, ro, by_owner, init_s, init_r, vp_s, vp_r, rv_s, rv_r, round_s, round_r, tr_s, tr_r, im_s, im_r, ft_s, ft_r, ou_s, ou_r, load_s, ip_s, ip_r, rl_s, rl_r, fe_s, fe_r,
         token_slab2, token_slab4, token_z, token_core, token_half, token_beside,
     ) = rest
     s = lax.axis_index("shot")
@@ -69,8 +69,6 @@
         copy.start()
         return copy
 
-    cross = [(dx, dr) for dr in range(-2, 3) for dx in (-1, 0, 1) if (dx, dr) != (0, 0)]
-
     barrier = pltpu.get_barrier_semaphore()
     zi = lax.rem(lax.div(s, 2), 8)
     pair = lax.rem(s, 16)
@@ -93,10 +91,6 @@
     loads = [pltpu.make_async_copy(hbm[at], loaded[at], load_s.at[at]) for at in range(12)]
     for at in (4, 1, 0, 3, 2, 5, 6, 7, 8, 9, 10, 11):
         loads[at].start()
-    loads[4].wait()
-    sv[...] = (vel[...] - MID).astype(BF16)
-    for at in (0, 1, 2, 3):
-        loads[at].wait()
     pl.semaphore_wait(barrier, len(peers))
     tell(token_slab2, [(s, slab_at(-2)), (s, slab_at(2))])
     tell(token_z, [(z_at(-2), b), (z_at(2), b)])
@@ -105,7 +99,7 @@
     first = ([], [])
 
     def send_first(f):
-        now, old = ((cur, prev), (acur, anext))[f]
+        now, old = ((hbm[1], hbm[0]), (acur, anext))[f]
         for side, step in ((0, 1), (1, -1)):
             target = slab_at(step)
             edge = pl.ds(4, 4) if step == 1 else pl.ds(0, 4)
@@ -113,12 +107,16 @@
             first[f].append(send(now.at[0], rc.at[side, f], *at, s, target))
             at = init_s.at[side, 2 * f + 1], init_r.at[side, 2 * f + 1]
             first[f].append(send(old.at[0, edge], rp.at[side, f], *at, s, target))
-            if f == 0:
-                first[f].append(send(sv.at[edge], rn.at[side], init_s.at[side, 4], init_r.at[side, 4], s, target))
+        for side, step in ((0, 1), (1, -1)) if f == 0 else ():
+            if side == 0:
+                loads[4].wait()
+                sv[...] = (vel[...] - MID).astype(BF16)
+            edge = pl.ds(4, 4) if step == 1 else pl.ds(0, 4)
+            first[f].append(send(sv.at[edge], rn.at[side], init_s.at[side, 4], init_r.at[side, 4], s, slab_at(step)))
 
     send_first(0)
 
-    for at in range(5, 12):
+    for at in (0, 1, 2, 3, *range(5, 12)):
         loads[at].wait()
     lane = lax.broadcasted_iota(jnp.int32, (64, 128), 1)
     diff = jnp.abs(lax.broadcasted_iota(jnp.int32, (128, 128), 0) - lax.broadcasted_iota(jnp.int32, (128, 128), 1))
@@ -185,7 +183,9 @@
     i, j, c = (q >> 3) & 3, (q >> 1) & 3, q & 1
     wanted = one_hot((iota(96, 64, 1) == (9 * i + 3 * j + (q >> 5)) * 2 + c) & (i < 3) & (j < 3))
     chosen = dot(wanted, taps_in).astype(BF16)
-    w1[...] = lax.dot_general(eye64, chosen, NT, preferred_element_type=F32).astype(BF16)
+    for k in range(3):
+        w1[64 * k:64 * k + 64, :] = lax.dot_general(
+            eye64, chosen[32 * k:32 * k + 32], NT, preferred_element_type=F32).astype(BF16)
     for k in range(3):
         for u in range(0, 9, 2):
             blocks = [wd[9 * (v % 3) + 3 * (v // 3) + k] for v in range(u, min(u + 2, 9))]
@@ -205,13 +205,19 @@
     bias_col = lax.dot_general(eye64, biases.astype(BF16), NT, preferred_element_type=F32)
     b1 = bias_col[:, 0:1] + bias_col[:, 1:2] + bias_col[:, 2:3]
     b2 = bias_col[:, 3:4] + bias_col[:, 4:5] + bias_col[:, 5:6]
-    r, col = iota(384, 144, 0), iota(384, 144, 1)
-    group = jnp.where(col >= 48, 1, 0) + jnp.where(col >= 96, 1, 0)
-    rest = col - 48 * group
-    part_of = rest >> 4
-    widen[...] = one_hot(
-        (((r >> 1) & 3) == group) & ((r & 1) == ((rest >> 3) & 1)) & (((r >> 3) & 3) < 3)
-        & (8 * part_of + (rest & 7) == (r >> 5) + ((r >> 3) & 3) + 5))
+    r, col = iota(32, 96, 0), iota(32, 96, 1)
+    group = jnp.where(col >= 32, 1, 0) + jnp.where(col >= 64, 1, 0)
+    rest = col - 32 * group
+    before, after = rest < 8, rest >= 24
+    edge_rest = jnp.where(after, rest - 24, rest)
+    channel = jnp.where(before | after, edge_rest >> 2, (rest - 8) >> 3)
+    plane_of = jnp.where(before, edge_rest & 3, jnp.where(after, 12 + (edge_rest & 3), 4 + ((rest - 8) & 7)))
+    fits = (((r >> 1) & 3) == group) & ((r & 1) == channel) & ((r >> 3) < 3)
+    shift = plane_of - (r >> 3) - 1
+    for x in range(12):
+        wide = dot(w1[...], one_hot(fits & (shift == x))).astype(BF16)
+        for k in range(3):
+            band1[k, 64 * x:64 * x + 64, :] = wide[64 * k:64 * k + 64]
 
     send_first(1)
     for slot, step in enumerate((2, 1, -1, -2)):
@@ -263,9 +269,10 @@
         g = dot(pick[...], jnp.concatenate(split(x, 3), axis=1))
         hot3 = jnp.concatenate([lane_hot[...]] * 3, axis=1)
         values = lax.dot_general(jnp.ones((8, 384), BF16), (g * hot3).astype(BF16), NT, preferred_element_type=F32)
-        tr[n:n + 1, :] = values[0:1, :]
-
-    tr[...] = jnp.zeros((8, 256), F32)
+        for part in range(2):
+            tr[2 * n + part:2 * n + part + 1, :] = values[0:1, 128 * part:128 * part + 128]
+
+    tr[8:16] = jnp.zeros((8, 128), F32)
     left, right = inside(-1), inside(1)
 
     def kappa_of(values, valid):
@@ -330,13 +337,15 @@
     pl.semaphore_wait(token_slab4, 2)
     pl.semaphore_wait(token_core, 1)
     tell(token_half, [(shot_at(16), b)])
+    for k in range(1, slabs):
+        send(tr.at[0:8], rt.at[k - 1], tr_s, tr_r, s, slab_at(k))
     round_of(1, 1)
     round_of(2, 0)
     pl.semaphore_wait(token_half, 1)
     tell(token_beside, [(s, slab_at(-1)), (s, slab_at(1))])
 
     for k in range(1, slabs):
-        send(tr, rt.at[k - 1], tr_s, tr_r, s, slab_at(k))
+        send(tr.at[8:16], rl.at[k - 1], rl_s, rl_r, s, slab_at(k))
     round_of(2, 1)
     image = hom[0] * lap[0]
     for n in range(1, STEPS):
@@ -349,12 +358,15 @@
         for slot, (base, valid) in enumerate(near_far):
             kap[base + plane] = kappa_of(rv[k - 1, slot] if k else vp[slot], valid)
     pltpu.make_async_copy(rt, rt, tr_r).wait()
-    total = tr[...]
+    pltpu.make_async_copy(rl, rl, rl_r).wait()
+    early, late = tr[0:8], tr[8:16]
     for k in range(slabs - 1):
-        total = total + rt[k]
+        early = early + rt[k]
+        late = late + rl[k]
     mf[...] = jnp.zeros((8, 256), F32)
     for n in range(STEPS):
-        trace = total[n:n + 1] - obs[n]
+        total, at = (early, 2 * n) if n < 4 else (late, 2 * n - 8)
+        trace = jnp.concatenate([total[at:at + 1], total[at + 1:at + 2]], axis=1) - obs[n]
         mis[n] = trace
         mf[n:n + 1, :] = trace
     amounts = jnp.zeros((256, 8), F32)
@@ -414,42 +426,52 @@
     centered = moved - CENTER
     for y in range(2):
         fs[y] = jnp.concatenate([centered[8 * y:8 * y + 8], update[8 * y:8 * y + 8]], axis=0).astype(BF16)
-
-    for slot, (dx, dr) in enumerate(cross):
-        send(fs, rf.at[slot], ft_s, ft_r, half + lax.rem(pair - dr + 16, 16), slab_at(-dx))
+    for side, first_plane in ((0, 4), (1, 0)):
+        fe[side] = jnp.concatenate(
+            [v[8 * y + first_plane:8 * y + first_plane + 4] for y in range(2) for v in (centered, update)],
+            axis=0).astype(BF16)
+
+    around = (-2, -1, 1, 2)
+    for slot, dr in enumerate(around):
+        send(fs, rf.at[slot], ft_s, ft_r, half + lax.rem(pair - dr + 16, 16), b)
+    for side, dx in ((0, -1), (1, 1)):
+        for dr in range(-2, 3):
+            send(fe.at[side], re.at[side, dr + 2], fe_s, fe_r, half + lax.rem(pair - dr + 16, 16), slab_at(-dx))
     pltpu.make_async_copy(rf, rf, ft_r).wait()
-    lane16 = iota(16, 128, 1)
-
-    def place_features(at, values):
-        feat[at, :, 0:128] = jnp.where(lane16 == 0, 0.0, pltpu.roll(values, 1, 1)).astype(BF16)
-        feat[at, :, 128:256] = values.astype(BF16)
-        feat[at, :, 256:384] = jnp.where(lane16 == 127, 0.0, pltpu.roll(values, 127, 1)).astype(BF16)
+    pltpu.make_async_copy(re, re, fe_r).wait()
+    lane32 = iota(32, 128, 1)
 
     def row_inside(k):
         return jnp.where((2 * pair + k >= 0) & (2 * pair + k < ROWS), 1.0, 0.0).astype(F32)
 
-    for slot, (dx, dr) in enumerate(cross):
-        valid = inside(dx) * row_inside(2 * dr)
+    for dr in range(-2, 3):
+        valid = row_inside(2 * dr)
+        beside = [re[side, dr + 2].astype(F32) * (valid * (left, right)[side]) for side in range(2)]
         for y in range(2):
-            place_features((2 * dr + 4 + y) * 3 + dx + 1, rf[slot, y].astype(F32) * valid)
-    for y in range(2):
-        place_features((4 + y) * 3 + 1, fs[y].astype(F32))
-
-    def first_conv(y, carry):
-        spread = dot(widen[...], feat[pl.ds(3 * y + 3, 9)].reshape(144, 384)).astype(BF16)
-        for k in range(3):
-            im[:, k] = spread[:, 128 * k:128 * k + 128].reshape(12, 32, 128)
-        row_ok = row_inside(y - 2)
-        for x0 in range(0, 12, 2):
-            g = dot(w1[...], jnp.concatenate([im[x0].reshape(96, 128), im[x0 + 1].reshape(96, 128)], axis=1))
-            for half in range(2):
-                plane = b * 8 + x0 + half - 2
-                ok = jnp.where((plane >= 0) & (plane < slabs * 8), row_ok, 0.0)
-                value = jnp.maximum(g[:, 128 * half:128 * half + 128] + b1, 0.0) * ok
-                h1[y, x0 + half] = value.astype(BF16)
+            own = fs[y].astype(F32) if dr == 0 else rf[around.index(dr), y].astype(F32) * valid
+            values = jnp.concatenate([beside[0][8 * y:8 * y + 8], own, beside[1][8 * y:8 * y + 8]], axis=0)
+            at = 2 * dr + 4 + y
+            feat[0, at] = jnp.where(lane32 == 0, 0.0, pltpu.roll(values, 1, 1)).astype(BF16)
+            feat[1, at] = values.astype(BF16)
+            feat[2, at] = jnp.where(lane32 == 127, 0.0, pltpu.roll(values, 127, 1)).astype(BF16)
+
+    def first_conv(i, carry):
+        rhs = [
+            jnp.concatenate([feat[k, pl.ds(2 * i + at + 1, 3)].reshape(96, 128) for at in range(2)], axis=1)
+            for k in range(3)]
+        for part in range(3):
+            rows = slice(256 * part, 256 * part + 256)
+            g = dot(band1[0, rows], rhs[0]) + dot(band1[1, rows], rhs[1]) + dot(band1[2, rows], rhs[2])
+            for at in range(2):
+                row_ok = row_inside(2 * i + at - 2)
+                for x in range(4):
+                    plane = b * 8 + 4 * part + x - 2
+                    ok = jnp.where((plane >= 0) & (plane < slabs * 8), row_ok, 0.0)
+                    value = jnp.maximum(g[64 * x:64 * x + 64, 128 * at:128 * at + 128] + b1, 0.0) * ok
+                    h1[2 * i + at, 4 * part + x] = value.astype(BF16)
         return carry
 
-    lax.fori_loop(0, 6, first_conv, 0)
+    lax.fori_loop(0, 3, first_conv, 0)
 
     def second_conv(y, carry):
         row_ok = row_inside(y - 1)
@@ -484,18 +506,21 @@
 
     for k in range(1, 16):
         send(row, ro.at[k - 1], ou_s, ou_r, half + lax.rem(pair + k, 16), b)
-    out[pair] = row[...]
+    by_owner[pair] = row[...]
     pltpu.make_async_copy(ro, ro, ou_r).wait()
     for k in range(1, 16):
-        out[lax.rem(pair - k + 16, 16)] = ro[k - 1]
+        by_owner[lax.rem(pair - k + 16, 16)] = ro[k - 1]
+    out[...] = jnp.swapaxes(by_owner[...].reshape(ROWS, 8, 128), 0, 1)
 
     for copy in sent:
         copy.wait_send()
     pltpu.make_async_copy(vp, vp, vp_s).wait()
     pltpu.make_async_copy(rv, rv, rv_s).wait()
     pltpu.make_async_copy(rt, rt, tr_s).wait()
+    pltpu.make_async_copy(rl, rl, rl_s).wait()
     pltpu.make_async_copy(ri.at[0:chips - 1], ri.at[0:chips - 1], im_s).wait()
     pltpu.make_async_copy(rf, rf, ft_s).wait()
+    pltpu.make_async_copy(re, re, fe_s).wait()
     pltpu.make_async_copy(ro, ro, ou_s).wait()
 
 
@@ -514,23 +539,23 @@
         f32(6, 8, 32, 128), f32(6, 8, 32, 128), f32(8, 32, 128), f32(2, 8, 16, 128), f32(8, 16, 128), f32(8, 16, 128),
         bf(8, 32, 128), bf(4, 32, 128), bf(7, 4, 32, 128), bf(2, 4, 32, 128), bf(2, 2, 8, 32, 128), bf(2, 2, 4, 32, 128),
         bf(2, 2, 8, 32, 128), bf(2, 2, 2, 8, 32, 128),
-        f32(8, 256), f32(slabs - 1, 8, 256), f32(8, 256),
+        f32(16, 128), f32(slabs - 1, 8, 128), f32(slabs - 1, 8, 128), f32(8, 256),
         bf(1536, 256), bf(256, 256), f32(256, 128), f32(32, 128), bf(256, 128), bf(128, 128),
-        f32(shots // 2, 16, 128), bf(2, 16, 128), bf(14, 2, 16, 128), bf(30, 16, 384),
-        f32(96, 64), bf(64, 96), bf(192, 576), bf(16, 576), bf(384, 144), bf(12, 3, 32, 128),
-        bf(6, 12, 64, 128), bf(4, 10, 64, 128), f32(16, 128), f32(15, 16, 128),
+        f32(shots // 2, 16, 128), bf(2, 16, 128), bf(2, 16, 128), bf(4, 2, 16, 128), bf(2, 5, 16, 128), bf(3, 10, 32, 128),
+        f32(96, 64), bf(192, 32), bf(192, 576), bf(16, 576), bf(3, 768, 96),
+        bf(6, 12, 64, 128), bf(4, 10, 64, 128), f32(16, 128), f32(15, 16, 128), f32(16, 16, 128),
         dma((2, 5)), dma((2, 5)), dma, dma, dma, dma, dma((4, 2)), dma((4, 2)),
-    ] + [dma] * 8 + [dma((12,)), dma, dma] + [pltpu.SemaphoreType.REGULAR] * 6
+    ] + [dma] * 8 + [dma((12,))] + [dma] * 6 + [pltpu.SemaphoreType.REGULAR] * 6
     rows, misfit = pl.pallas_call(
         functools.partial(kernel, slabs, shots),
-        out_shape=(jax.ShapeDtypeStruct((16, 16, 128), F32), jax.ShapeDtypeStruct((STEPS, 1, 256), F32)),
+        out_shape=(jax.ShapeDtypeStruct(velocity.shape, F32), jax.ShapeDtypeStruct((STEPS, 1, 256), F32)),
         in_specs=[smem, smem, smem] + [pl.BlockSpec(memory_space=pl.ANY)] * 12,
         out_specs=(vmem, vmem),
         scratch_shapes=scratch,
         compiler_params=pltpu.CompilerParams(
             collective_id=0, has_side_effects=True, vmem_limit_bytes=60 * 1024 * 1024),
     )(wavelet, source_cell, bias_out, *arrays)
-    return jnp.swapaxes(rows.reshape(ROWS, 8, 128), 0, 1), jnp.swapaxes(misfit, 0, 1)
+    return rows, jnp.swapaxes(misfit, 0, 1)
 
 
 def solution(mesh):

time: 83.7 us -> 81.1 us (0.969)
  Pallas kernels: 79.4 us -> 76.9 us
    pallas_call x1, Pallas kernels: 79.4 us -> 76.9 us  [shards(): pl.pallas_call(functools.partial(kernel, slabs, shots), out_shape=(jax.Sh...]
    reshape x1 -> x0, local copies, waits for them, and re-layouts: 1.59 us -> none  [shards(): rows.reshape(ROWS, 8, 128)]
    unnamed x3 -> x4, local copies, waits for them, and re-layouts: 0.6 us -> 2.17 us
where the time goes in v4:
time: 81.1 us; the launch traced here: 81 us
  Pallas kernels  76.9 us (95%)
  local copies, waits for them, and re-layouts  2.17 us (3%)
  between operations  1.94 us (2%)
    pallas_call x1, Pallas kernels, shards(): pl.pallas_call(functools.partial(kernel, slabs, shots), out_shape=(jax.Sh...  76.9 us
    unnamed x4, local copies, waits for them, and re-layouts  2.17 us

profile of v4, /device:TPU:1, one launch (start us, length us, event | category | flops | bytes accessed | tf_op | source)
XLA Modules:
  0.0 81.0 jit_solution(12195871544690146720)
XLA Ops:
  1.9 76.9 %shard_map.158 = (f32[8,32,128]{2,1,0:T(8,128)}, f32[6,1,256]{2,1,0:T(1,128)}) custom-call(f32[1,6]{1,0:T(1,128)} %wav.1, s32[1]{0:T(128)S(6)} %copy.19.src, f32[1]{0:T(128)S(6)} %copy.20.b3, bf16[1,8,32,128]{3,2,1,0:T(8,128)(2,1)} %refs_0_.1, bf16[1,8,32,128]{3,2,1,0:T(8,128)(2,1)} %refs_1_.1, bf16[1,8,32,128]{3,2,1,0:T(8,128)(2,1)} %refs_2_.1, ...), custom_call_target="tpu_custom_call" | custom-call | tf_op jit(solution)/shard_map/pallas_call | solution.py:549
  78.8 0.0 copy-start
  78.8 1.6 %copy.21 = f32[8,32,128]{2,1,0:T(8,128)} copy(f32[8,32,128]{2,1,0:T(8,128)} %get-tuple-element.8) | data formatting | bytes 262144
  80.4 0.0 copy-done
  80.4 0.6 copy.22
Async XLA Ops:
  78.8 1.6 %copy-start = (f32[6,1,256]{2,1,0:T(1,128)S(1)}, f32[6,1,256]{2,1,0:T(1,128)}, u32[]{:S(2)}) copy-start(f32[6,1,256]{2,1,0:T(1,128)} %get-tuple-element.5) | copy-start | bytes 18436

commit v5 on v4

--- a/solution.py
+++ b/solution.py
@@ -47,7 +47,7 @@
     hbm, (out, mis), loaded, rest = refs[:12], refs[12:14], refs[14:26], refs[26:]
     prev, cur, anext, acur, vel, rec, obs, wi, bi, wd, bd, wo = loaded
     (
-        u0, u1, wa0, wa1, da, db, zs, js, kap, lap, hom, img, imgt, ip, chip_sum, sv, vp, rv, rn, rc, rp, sb, rb, tr, rt, rl, mf, hot, pick, lane_hot, src_hot, bands, bandl, ri, fs, fe, rf, re, feat, wf, w1, wm, w3, band1, h1, h2, row, ro, by_owner, init_s, init_r, vp_s, vp_r, rv_s, rv_r, round_s, round_r, tr_s, tr_r, im_s, im_r, ft_s, ft_r, ou_s, ou_r, load_s, ip_s, ip_r, rl_s, rl_r, fe_s, fe_r,
+        u0, u1, wa0, wa1, da, db, zs, js, kap, lap, hom, img, imgt, ip, chip_sum, sv, vp, rv, rn, rc, rp, sb, rb, tr, rt, rl, mf, hot, pick, lane_hot, src_hot, bands, bandl, ri, fs, fe, rf, re, feat, wf, w1, wm, w3, band1, h1, h2, taps, row, ro, by_owner, init_s, init_r, vp_s, vp_r, rv_s, rv_r, round_s, round_r, tr_s, tr_r, im_s, im_r, ft_s, ft_r, ou_s, ou_r, load_s, ip_s, ip_r, rl_s, rl_r, fe_s, fe_r,
         token_slab2, token_slab4, token_z, token_core, token_half, token_beside,
     ) = rest
     s = lax.axis_index("shot")
@@ -191,13 +191,10 @@
             blocks = [wd[9 * (v % 3) + 3 * (v // 3) + k] for v in range(u, min(u + 2, 9))]
             both = lax.dot_general(eye64, jnp.concatenate(blocks, axis=0), NT, preferred_element_type=F32)
             wm[64 * k:64 * k + 64, 64 * u:64 * (u + len(blocks))] = both.astype(BF16)
-    for u in range(0, 9, 2):
-        both = jnp.zeros((16, 128), F32)
-        for v in range(u, min(u + 2, 9)):
-            wanted = one_hot((iota(16, 32, 1) == 9 * (v % 3) + 3 * (v // 3) + iota(16, 32, 0)) & (iota(16, 32, 0) < 3))
-            place = one_hot(iota(64, 128, 1) == iota(64, 128, 0) + 64 * (v - u))
-            both = both + dot(dot(wanted, taps_out).astype(BF16), place)
-        w3[:, 64 * u:min(64 * u + 128, 576)] = both[:, 0:min(128, 576 - 64 * u)].astype(BF16)
+    u, k = iota(80, 32, 0) >> 3, iota(80, 32, 0) & 7
+    j = jnp.where(u >= 3, 1, 0) + jnp.where(u >= 6, 1, 0)
+    wanted = one_hot((iota(80, 32, 1) == 9 * (u - 3 * j) + 3 * j + k) & (k < 3) & (u < 9))
+    w3[...] = dot(wanted, taps_out).astype(BF16)
     sub64 = iota(8, 64, 0)
     biases = jnp.zeros((8, 64), F32)
     for at, part in enumerate(split(bi[...], 3) + split(bd[...], 3)):
@@ -346,17 +343,17 @@
 
     for k in range(1, slabs):
         send(tr.at[8:16], rl.at[k - 1], rl_s, rl_r, s, slab_at(k))
-    round_of(2, 1)
-    image = hom[0] * lap[0]
-    for n in range(1, STEPS):
-        image = image + hom[n] * lap[n]
-    img[...] = image
     pltpu.make_async_copy(rv, rv, rv_r).wait()
     near_far = ((0, inside(-2)), (8, left), (24, right), (32, inside(2)))
     for k in range(8):
         plane = lax.rem(zi - k + 8, 8)
         for slot, (base, valid) in enumerate(near_far):
             kap[base + plane] = kappa_of(rv[k - 1, slot] if k else vp[slot], valid)
+    round_of(2, 1)
+    image = hom[0] * lap[0]
+    for n in range(1, STEPS):
+        image = image + hom[n] * lap[n]
+    img[...] = image
     pltpu.make_async_copy(rt, rt, tr_r).wait()
     pltpu.make_async_copy(rl, rl, rl_r).wait()
     early, late = tr[0:8], tr[8:16]
@@ -491,18 +488,20 @@
     lax.fori_loop(0, 4, second_conv, 0)
 
     lane1 = lax.broadcasted_iota(jnp.int32, (1, 128), 1)
+    for y in range(4):
+        for x in range(0, 10, 2):
+            g = dot(w3[...], jnp.concatenate([h2[y, x], h2[y, x + 1]], axis=1))
+            taps[y, x] = g[0:72, 0:128]
+            taps[y, x + 1] = g[0:72, 128:256]
     for y in range(2):
-        for x in range(0, 8, 2):
-            halves = []
-            for at in (x, x + 1):
-                halves.append(jnp.concatenate([h2[y + j, at:at + 3].reshape(192, 128) for j in range(3)], axis=0))
-            pair_g = dot(w3[...], jnp.concatenate(halves, axis=1))
-            for at in range(2):
-                g = pair_g[0:8, 128 * at:128 * at + 128]
-                low = jnp.where(lane1 == 0, 0.0, pltpu.roll(g, 1, 1)[0:1])
-                high = jnp.where(lane1 == 127, 0.0, pltpu.roll(g, 127, 1)[2:3])
-                i = 8 * y + x + at
-                row[i:i + 1, :] = moved[i:i + 1] + (g[1:2] + low + high + b3[0])
+        for x in range(8):
+            g = taps[y, x, 0:8]
+            for u in range(1, 9):
+                g = g + taps[y + u // 3, x + u % 3, 8 * u:8 * u + 8]
+            low = jnp.where(lane1 == 0, 0.0, pltpu.roll(g, 1, 1)[0:1])
+            high = jnp.where(lane1 == 127, 0.0, pltpu.roll(g, 127, 1)[2:3])
+            i = 8 * y + x
+            row[i:i + 1, :] = moved[i:i + 1] + (g[1:2] + low + high + b3[0])
 
     for k in range(1, 16):
         send(row, ro.at[k - 1], ou_s, ou_r, half + lax.rem(pair + k, 16), b)
@@ -542,8 +541,8 @@
         f32(16, 128), f32(slabs - 1, 8, 128), f32(slabs - 1, 8, 128), f32(8, 256),
         bf(1536, 256), bf(256, 256), f32(256, 128), f32(32, 128), bf(256, 128), bf(128, 128),
         f32(shots // 2, 16, 128), bf(2, 16, 128), bf(2, 16, 128), bf(4, 2, 16, 128), bf(2, 5, 16, 128), bf(3, 10, 32, 128),
-        f32(96, 64), bf(192, 32), bf(192, 576), bf(16, 576), bf(3, 768, 96),
-        bf(6, 12, 64, 128), bf(4, 10, 64, 128), f32(16, 128), f32(15, 16, 128), f32(16, 16, 128),
+        f32(96, 64), bf(192, 32), bf(192, 576), bf(80, 64), bf(3, 768, 96),
+        bf(6, 12, 64, 128), bf(4, 10, 64, 128), f32(4, 10, 72, 128), f32(16, 128), f32(15, 16, 128), f32(16, 16, 128),
         dma((2, 5)), dma((2, 5)), dma, dma, dma, dma, dma((4, 2)), dma((4, 2)),
     ] + [dma] * 8 + [dma((12,))] + [dma] * 6 + [pltpu.SemaphoreType.REGULAR] * 6
     rows, misfit = pl.pallas_call(

time: 81.1 us -> 81.1 us (level)
  no operation moved by 1% of the time
where the time goes in v5:
time: 81.1 us; the launch traced here: 80.9 us
  Pallas kernels  76.8 us (95%)
  local copies, waits for them, and re-layouts  2.17 us (3%)
  between operations  1.94 us (2%)
    pallas_call x1, Pallas kernels, shards(): pl.pallas_call(functools.partial(kernel, slabs, shots), out_shape=(jax.Sh...  76.8 us
    unnamed x4, local copies, waits for them, and re-layouts  2.17 us

profile of v5, /device:TPU:1, one launch (start us, length us, event | category | flops | bytes accessed | tf_op | source)
XLA Modules:
  0.0 80.9 jit_solution(9268626307813021949)
XLA Ops:
  1.9 76.8 %shard_map.158 = (f32[8,32,128]{2,1,0:T(8,128)}, f32[6,1,256]{2,1,0:T(1,128)}) custom-call(f32[1,6]{1,0:T(1,128)} %wav.1, s32[1]{0:T(128)S(6)} %copy.19.src, f32[1]{0:T(128)S(6)} %copy.20.b3, bf16[1,8,32,128]{3,2,1,0:T(8,128)(2,1)} %refs_0_.1, bf16[1,8,32,128]{3,2,1,0:T(8,128)(2,1)} %refs_1_.1, bf16[1,8,32,128]{3,2,1,0:T(8,128)(2,1)} %refs_2_.1, ...), custom_call_target="tpu_custom_call" | custom-call | tf_op jit(solution)/shard_map/pallas_call | solution.py:548
  78.7 0.0 copy-start
  78.7 1.6 %copy.21 = f32[8,32,128]{2,1,0:T(8,128)} copy(f32[8,32,128]{2,1,0:T(8,128)} %get-tuple-element.8) | data formatting | bytes 262144
  80.3 0.0 copy-done
  80.3 0.6 copy.22
Async XLA Ops:
  78.7 1.6 %copy-start = (f32[6,1,256]{2,1,0:T(1,128)S(1)}, f32[6,1,256]{2,1,0:T(1,128)}, u32[]{:S(2)}) copy-start(f32[6,1,256]{2,1,0:T(1,128)} %get-tuple-element.5) | copy-start | bytes 18436
